TPU v7x, 128 devices: a whole 4x4x4 slice. The times are simulated.
128 devices in a mesh: ctx: 16 (over x_lo, z, core), ch: 4 (over y), rep: 2 (over x_hi).
Axes of the slice: x: 4 (x_hi: 2, x_lo: 2; x = x_hi * 2 + x_lo), y: 4, z: 4, core: 2. Of those that a mesh axis runs over, the one named last changes fastest.
Arguments:
- saved_input: bfloat16 [2, 8192, 8192], P('rep', 'ctx', 'ch'), may hold values from -6 to 6
- out_grad: bfloat16 [2, 8192, 8192], P('rep', 'ctx', 'ch'), may hold values from -6 to 6
- filter_taps: bfloat16 [256, 8192], P('ctx', 'ch'), may hold values from -0.375 to 0.375
- valid_counts: int32 [2, 16], P('rep', 'ctx'), may hold values from 128 to 512
Outputs:
- input_grad: bfloat16 [2, 8192, 8192], P('rep', 'ctx', 'ch')
- tap_grad: float32 [256, 8192], P('ctx', 'ch')
Inputs may be any that keep to these rules, and one draw needn't show every extreme that they name: `valid_counts`: positions of a block at local index below its count are live; the others carry no gradient.
All inputs are finite; a program needn't handle non-finite values.
Results may differ from a plain program's by a relative error of at most 0.001.
Values may be sent and summed in bfloat16 or wider, within the bound.
A program may use at most 128 MiB of HBM per device.

v0:
```python
import math

import jax
import jax.numpy as jnp
from jax import lax
from jax.sharding import PartitionSpec as P

REACH = 128


def with_halo(cells, sides, width):
    for axis, dim in sides:
        count = lax.axis_size(axis)
        ends = count - 1
        head = lax.slice_in_dim(cells, 0, width, axis=dim)
        tail = lax.slice_in_dim(cells, cells.shape[dim] - width, cells.shape[dim], axis=dim)
        cells = jnp.concatenate(
            [
                lax.ppermute(tail, axis, [(i, (i + 1) % count) for i in range(ends)]),
                cells,
                lax.ppermute(head, axis, [((i + 1) % count, i) for i in range(ends)]),
            ],
            axis=dim,
        )
    return cells


def correlate(signal, taps, out_len):
    tap_count = taps.shape[0]
    channels = taps.shape[1]
    row_block = math.gcd(32, out_len)
    block_count = out_len // row_block
    window = row_block + tap_count
    needed = out_len + tap_count
    present = signal.shape[0]
    if present < needed:
        signal = jnp.concatenate([signal, jnp.zeros((needed - present, channels), signal.dtype)], 0)
    else:
        pass
    lane_width = min(128, channels)

    def one_group(block_index, running):
        column = block_index * lane_width
        signal_part = lax.dynamic_slice_in_dim(signal, column, lane_width, 1)
        tap_part = lax.dynamic_slice_in_dim(taps, column, lane_width, 1)
        extended = jnp.concatenate(
            [tap_part, jnp.zeros((row_block + 1, lane_width), tap_part.dtype)], 0
        )
        flattened = jnp.tile(extended, (row_block, 1))[: row_block * window]
        toeplitz = flattened.reshape(row_block, window, lane_width)
        windows = jnp.stack(
            [
                signal_part[row_block * offset : row_block * offset + window]
                for offset in range(block_count)
            ]
        )
        product = jnp.einsum("bjc,ajc->abc", toeplitz, windows, preferred_element_type=jnp.float32)
        return lax.dynamic_update_slice_in_dim(
            running, product.reshape(out_len, lane_width), column, 1
        )

    return lax.fori_loop(
        0, channels // lane_width, one_group, jnp.zeros((out_len, channels), jnp.float32)
    )


def local(saved_input, out_grad, filter_taps, valid_counts):
    block_rows = saved_input.shape[1]
    live_rows = (jnp.arange(block_rows) < valid_counts[0, 0]).astype(jnp.bfloat16)[:, None]
    stacked = jnp.stack([saved_input[0] * live_rows, out_grad[0] * live_rows])
    padded = with_halo(stacked, (("ctx", 1),), REACH)
    input_padded = padded[0]
    grad_padded = padded[1]
    whole_taps = lax.all_gather(filter_taps, "ctx", axis=0, tiled=True)
    running = correlate(grad_padded, whole_taps, block_rows)
    scale = 1.0 / math.sqrt(block_rows * lax.axis_size("ctx") * lax.axis_size("rep"))
    reversed_terms = correlate(input_padded[1:], stacked[1], 2 * REACH)
    tap_terms = reversed_terms[::-1] * scale
    segment = lax.psum_scatter(tap_terms, "ctx", scatter_dimension=0, tiled=True)
    tap_grad = lax.psum(segment, "rep")
    input_grad = (running * live_rows.astype(jnp.float32)).astype(jnp.bfloat16)[None]
    return (input_grad, tap_grad)


def solution(mesh):
    return jax.shard_map(
        local,
        mesh=mesh,
        in_specs=(P("rep", "ctx", "ch"), P("rep", "ctx", "ch"), P("ctx", "ch"), P("rep", "ctx")),
        out_specs=(P("rep", "ctx", "ch"), P("ctx", "ch")),
        check_vma=False,
    )
```

profile of v0, /device:TPU:0, one launch (start us, length us, event | category | flops | bytes accessed | tf_op | source)
XLA Modules:
  0.0 1237.1 jit_solution(18372715880683644175)
XLA Ops:
  21.1 6.6 pad_maximum_fusion
  34.1 651.3 %while.27 = (s32[]{:T(128)}, f32[256,2048]{1,0:T(8,128)}, bf16[768,2048]{1,0:T(8,128)(2,1)}, bf16[512,2048]{1,0:T(8,128)(2,1)}, s32[]{:T(128)}, /*index=5*/s32[]...) while((s32[]{:T(128)}, f32[256,2048]{1,0:T(8,128)}, ...), condition=%wide.region_3.0_spmd, body=%wide.region_2.0_spmd.sunk | while | flops 35651596 | bytes 44802888 | solution.py:62
  39.3 7.1 stack.191
  50.1 5.4 tile.49
  60.7 9.0 copy.684
  80.0 7.1 stack.191
  90.8 5.4 tile.49
  101.4 9.0 copy.684
  120.7 7.1 stack.191
  131.5 5.4 tile.49
  142.1 9.0 copy.684
  161.6 7.1 stack.191
  172.3 5.4 tile.49
  182.9 9.0 copy.684
  202.2 7.1 stack.191
  223.6 9.0 copy.684
  242.8 7.1 stack.191
  253.6 5.4 tile.49
  264.2 9.0 copy.684
  283.4 7.1 stack.191
  294.2 5.4 tile.49
  304.8 9.0 copy.684
  324.3 7.1 stack.191
  335.1 5.4 tile.49
  345.7 9.0 copy.684
  365.3 7.1 stack.191
  376.1 5.4 tile.49
  386.7 9.0 copy.684
  405.9 7.1 stack.191
  427.3 9.0 copy.684
  446.6 7.1 stack.191
  467.9 9.0 copy.684
  487.2 7.1 stack.191
  498.0 5.4 tile.49
  508.6 9.0 copy.684
  527.9 7.1 stack.191
  549.3 9.0 copy.684
  568.5 7.1 stack.191
  579.3 5.4 tile.49
  589.9 9.0 copy.684
  609.2 7.1 stack.191
  620.0 5.4 tile.49
  630.6 9.0 copy.684
  649.9 7.1 stack.191
  671.3 9.0 copy.684
  685.4 13.7 %rev.3 = f32[256,2048]{1,0:T(8,128)S(1)} reverse(f32[256,2048]{1,0:T(8,128)} %get-tuple-element.161), dimensions={0} | reverse | bytes 4194304 | tf_op jit(solution)/shard_map/rev | solution.py:78
  707.3 477.1 %while.26 = (s32[]{:T(128)}, f32[512,2048]{1,0:T(8,128)}, bf16[768,2048]{1,0:T(8,128)(2,1)}, bf16[256,2048]{1,0:T(8,128)(2,1)}, s32[]{:T(128)}, /*index=5*/s32[]...) while((s32[]{:T(128)}, f32[512,2048]{1,0:T(8,128)}, ...), condition=%wide.region_1.0_spmd, body=%wide.region_0.0_spmd.sunk | while | flops 37748756 | bytes 28812296 | solution.py:62
  712.3 8.5 stack.190
  742.2 8.5 stack.190
  772.2 8.5 stack.190
  802.2 8.5 stack.190
  832.1 8.5 stack.190
  862.0 8.5 stack.190
  891.6 8.5 stack.190
  921.3 8.5 stack.190
  951.1 8.5 stack.190
  980.8 8.5 stack.190
  1010.9 8.5 stack.190
  1040.8 8.5 stack.190
  1070.5 8.5 stack.190
  1100.3 8.5 stack.190
  1130.0 8.5 stack.190
  1159.9 8.5 stack.190
  1188.2 40.9 %all-reduce.5.cloned.1.call-done = f32[16,2048]{1,0:T(8,128)} async-done(((f32[16,2048]{1,0:T(8,128)}), f32[16,2048]{1,0:T(8,128)}) %all-reduce.5.cloned.1.call-update) | async-done | bytes 131088 | tf_op jit(solution)/shard_map/psum | solution.py:80
  (708 shorter events, 706.2 us)
Async XLA Ops:
  7.2 697.6 %all-gather.2.cloned.1.call-start = ((), (), s32[]{:S(2)}) async-start(), calls=%async_computation.1 | async-start | bytes 1114112 | tf_op jit(solution)/shard_map/all_gather | solution.py:74
  10.4 2.0 copy-start.1
  12.4 8.7 collective-permute-start.1
  13.7 7.4 collective-permute-start
  17.8 1166.6 %reduce-scatter.2.cloned.1.call-start = ((), (), s32[]{:S(2)}) async-start(), calls=%async_computation.2 | async-start | bytes 2228224 | tf_op jit(solution)/shard_map/reduce_scatter | solution.py:79
  17.8 3.3 copy-start.2
  27.8 2.6 copy-start
  704.5 524.5 %all-reduce.5.cloned.1.call-start = ((), (), s32[]{:S(2)}) async-start(), calls=%async_computation.3 | async-start | bytes 262144 | tf_op jit(solution)/shard_map/psum | solution.py:80
Sparse Core Ops, SparseCore 0:
  17.9 36.8 all-gather.1
  704.7 78.5 reduce-scatter.1
  1184.5 44.5 all-reduce.4
where the time goes:
time: 1260 us; the launch traced here: 1240 us
  local copies, waits for them, and re-layouts  1030 us (82%)
  matrix products  124 us (10%)
  waiting for transfers between devices  41 us (3%)
  other arithmetic  19.4 us (2%)
  between operations  14.5 us (1%)
    another operation x448, local copies, waits for them, and re-layouts, one_group(): jnp.stack([signal_part[row_block * offset:row_block * offset + window] fo...  417 us
    reshape x32, local copies, waits for them, and re-layouts, one_group(): toeplitz = flattened.reshape(row_block, window, lane_width)  204 us
    another operation x64, local copies, waits for them, and re-layouts, one_group(): flattened = jnp.tile(extended, (row_block, 1))[:row_block * window]  171 us
    slice x32, local copies, waits for them, and re-layouts, one_group(): flattened = jnp.tile(extended, (row_block, 1))[:row_block * window]  129 us
    dot_general x32, matrix products, one_group(): jnp.einsum('bjc,ajc->abc', toeplitz, windows, preferred_element_type=jnp....  124 us
    psum x1, waiting for transfers between devices, local(): tap_grad = lax.psum(segment, 'rep')  40.9 us
    transpose x32, local copies, waits for them, and re-layouts, one_group(): jnp.einsum('bjc,ajc->abc', toeplitz, windows, preferred_element_type=jnp....  29.1 us
    dynamic_slice x32, local copies, waits for them, and re-layouts, one_group(): tap_part = lax.dynamic_slice_in_dim(taps, column, lane_width, 1)  28.2 us
  transfers between devices with their start and end apart: 5, of which 1 were waited for; matrix products, arithmetic and copies ran while one was open for 94% of the time, Pallas kernels for 0%

commit v1 on v0

v1 whole, which is shorter than its diff:
```python
import math

import jax
import jax.numpy as jnp
import numpy as np
from jax import lax
from jax.experimental import pallas as pl
from jax.experimental.pallas import tpu as pltpu
from jax.sharding import PartitionSpec as P

REACH = 128
TILE = 256


def transform_tables():
    order = np.concatenate([np.arange(0, 128, 2), np.arange(1, 128, 2)])
    turns = (2 * order[:, None] + 1) * np.arange(128)[None, :] % 512
    angle = np.pi * turns / 256.0
    forward = np.concatenate([np.cos(angle), -np.sin(angle)], 0)
    high = forward.astype(jnp.bfloat16)
    low = (forward - high.astype(np.float64)).astype(jnp.bfloat16)
    analysis = np.concatenate([high, low], 1)
    inv_high = (high.astype(np.float64).T / 128).astype(jnp.bfloat16)
    inv_low = (low.astype(np.float64).T / 128).astype(jnp.bfloat16)
    synthesis = np.concatenate([inv_high, inv_high, inv_low], 1)
    return analysis, synthesis


def split(value):
    high = value.astype(jnp.bfloat16)
    low = (value - high.astype(jnp.float32)).astype(jnp.bfloat16)
    return high, low


def kernel(count_ref, ana_ref, syn_ref, x_ref, g_ref, left_ref, right_ref, w_ref,
           out_ref, tap_ref, a_ref, xf_ref, wf_ref, y_ref, t_ref):
    live_count = count_ref[0, 0]
    ana = ana_ref[...]
    syn = syn_ref[...]

    def analyse(block):
        return jnp.dot(ana, jnp.concatenate([block, block], 0), preferred_element_type=jnp.float32)

    def live_rows(b):
        rows = lax.broadcasted_iota(jnp.int32, (REACH, TILE), 0) + b * REACH
        return rows < live_count

    a_ref[0] = analyse(left_ref[...])
    a_ref[5] = analyse(right_ref[...])
    for b in range(4):
        live = live_rows(b)
        rows = pl.ds(b * REACH, REACH)
        a_ref[b + 1] = analyse(jnp.where(live, g_ref[rows, :], 0))
        xf_ref[b] = analyse(jnp.where(live, x_ref[rows, :], 0))
    for h in range(2):
        wf_ref[h] = analyse(w_ref[pl.ds(h * REACH, REACH), :])

    step = 16
    for chunk in range(128 // step):
        re = pl.ds(chunk * step, step)
        im = pl.ds(128 + chunk * step, step)
        positive = chunk * step < 64
        ar = [a_ref[b, re, :] for b in range(6)]
        ai = [a_ref[b, im, :] for b in range(6)]
        gr, gi = [], []
        for b in range(5):
            if positive:
                gr.append(ar[b] + ai[b + 1])
                gi.append(ai[b] - ar[b + 1])
            else:
                gr.append(ar[b] - ai[b + 1])
                gi.append(ai[b] + ar[b + 1])
        for h in range(2):
            tr = ti = None
            for b in range(4):
                xr, xi = xf_ref[b, re, :], xf_ref[b, im, :]
                pr = xr * gr[b + h] + xi * gi[b + h]
                pi = xr * gi[b + h] - xi * gr[b + h]
                tr, ti = (pr, pi) if tr is None else (tr + pr, ti + pi)
            for rows, val in ((chunk * step, tr), (128 + chunk * step, ti)):
                high, low = split(val)
                t_ref[h, pl.ds(rows, step), :] = high
                t_ref[h, pl.ds(256 + rows, step), :] = low
                t_ref[h, pl.ds(512 + rows, step), :] = high
        w0r, w0i = wf_ref[0, re, :], wf_ref[0, im, :]
        w1r, w1i = wf_ref[1, re, :], wf_ref[1, im, :]
        for b in range(4):
            yr = (w0r * gr[b] + w0i * gi[b]) + (w1r * gr[b + 1] + w1i * gi[b + 1])
            yi = (w0r * gi[b] - w0i * gr[b]) + (w1r * gi[b + 1] - w1i * gr[b + 1])
            for rows, val in ((chunk * step, yr), (128 + chunk * step, yi)):
                high, low = split(val)
                y_ref[b, pl.ds(rows, step), :] = high
                y_ref[b, pl.ds(256 + rows, step), :] = low
                y_ref[b, pl.ds(512 + rows, step), :] = high

    for h in range(2):
        tap_ref[pl.ds(h * REACH, REACH), :] = jnp.dot(
            syn, t_ref[h], preferred_element_type=jnp.float32) * (1.0 / 128)
    for b in range(4):
        value = jnp.dot(syn, y_ref[b], preferred_element_type=jnp.float32)
        out_ref[pl.ds(b * REACH, REACH), :] = jnp.where(live_rows(b), value, 0).astype(jnp.bfloat16)


def convolve(counts, x, g, left, right, taps):
    rows, channels = x.shape
    ana, syn = transform_tables()
    block = lambda n: pl.BlockSpec((n, TILE), lambda i: (0, i))
    whole = lambda a: pl.BlockSpec(a.shape, lambda i: (0, 0))
    return pl.pallas_call(
        kernel,
        grid=(channels // TILE,),
        out_shape=(jax.ShapeDtypeStruct((rows, channels), jnp.bfloat16),
                   jax.ShapeDtypeStruct((2 * REACH, channels), jnp.float32)),
        in_specs=[pl.BlockSpec(memory_space=pltpu.SMEM), whole(ana), whole(syn),
                  block(rows), block(rows), block(REACH), block(REACH), block(2 * REACH)],
        out_specs=(block(rows), block(2 * REACH)),
        scratch_shapes=[
            pltpu.VMEM((6, 256, TILE), jnp.float32),
            pltpu.VMEM((4, 256, TILE), jnp.float32),
            pltpu.VMEM((2, 256, TILE), jnp.float32),
            pltpu.VMEM((4, 768, TILE), jnp.bfloat16),
            pltpu.VMEM((2, 768, TILE), jnp.bfloat16),
        ],
        compiler_params=pltpu.CompilerParams(vmem_limit_bytes=40 << 20),
    )(counts, jnp.asarray(ana), jnp.asarray(syn), x, g, left, right, taps)


def local(saved_input, out_grad, filter_taps, valid_counts):
    block_rows = saved_input.shape[1]
    count = lax.axis_size("ctx")
    grad = out_grad[0]
    live = (jnp.arange(block_rows) < valid_counts[0, 0])[:, None]
    head = jnp.where(live[:REACH], grad[:REACH], 0)
    tail = jnp.where(live[-REACH:], grad[-REACH:], 0)
    left = lax.ppermute(tail, "ctx", [(i, i + 1) for i in range(count - 1)])
    right = lax.ppermute(head, "ctx", [(i + 1, i) for i in range(count - 1)])
    taps = lax.all_gather(filter_taps, "ctx", axis=0, tiled=True)
    input_grad, tap_terms = convolve(valid_counts, saved_input[0], grad, left, right, taps)
    segment = lax.psum_scatter(tap_terms, "ctx", scatter_dimension=0, tiled=True)
    tap_grad = lax.psum(segment, "rep")
    return (input_grad[None], tap_grad)


def solution(mesh):
    return jax.shard_map(
        local,
        mesh=mesh,
        in_specs=(P("rep", "ctx", "ch"), P("rep", "ctx", "ch"), P("ctx", "ch"), P("rep", "ctx")),
        out_specs=(P("rep", "ctx", "ch"), P("ctx", "ch")),
        check_vma=False,
    )
```

time: 1260 us -> 167 us (0.13); the launches traced: 1240 us -> 167 us
  local copies, waits for them, and re-layouts: 1030 us -> 7.57 us
  matrix products: 124 us -> 0 us
  waiting for transfers between devices: 41 us -> 125 us
  other arithmetic: 19.4 us -> 1.34 us
  Pallas kernels: 0 us -> 13.8 us
    another operation x512 -> x0, local copies, waits for them, and re-layouts: 587 us -> none  [the longest x448 417 us: one_group(): jnp.stack([signal_part[row_block * offset:row_block * offset + window] fo...]
    reshape x32 -> x0, local copies, waits for them, and re-layouts: 204 us -> none  [one_group(): toeplitz = flattened.reshape(row_block, window, lane_width)]
    slice x33 -> x1, local copies, waits for them, and re-layouts: 130 us -> 0.01 us  [local(): head = jnp.where(live[:REACH], grad[:REACH], 0)]
    dot_general x32 -> x0, matrix products: 124 us -> none  [one_group(): jnp.einsum('bjc,ajc->abc', toeplitz, windows, preferred_element_type=jnp....]
    reduce_scatter x1, waiting for transfers between devices: 0.01 us -> 63.3 us  [local(): lax.psum_scatter(tap_terms, 'ctx', scatter_dimension=0, tiled=True)]
    transpose x32 -> x0, local copies, waits for them, and re-layouts: 29.1 us -> none  [one_group(): jnp.einsum('bjc,ajc->abc', toeplitz, windows, preferred_element_type=jnp....]
    all_gather x1, waiting for transfers between devices: 0.02 us -> 29.1 us  [local(): taps = lax.all_gather(filter_taps, 'ctx', axis=0, tiled=True)]
    dynamic_slice x32 -> x0, local copies, waits for them, and re-layouts: 28.2 us -> none  [one_group(): tap_part = lax.dynamic_slice_in_dim(taps, column, lane_width, 1)]
  transfers between devices with their start and end apart: 5 -> 5, of which waited for: 1 -> 4; matrix products, arithmetic and copies ran while one was open for 94% -> 1% of each run, Pallas kernels for 0% -> 0%
where the time goes in v1:
time: 167 us
  waiting for transfers between devices  125 us (75%)
  between operations  14.4 us (9%)
  Pallas kernels  13.8 us (8%)
  local copies, waits for them, and re-layouts  7.57 us (5%)
  starting transfers between devices  4.47 us (3%)
    reduce_scatter x1, waiting for transfers between devices, local(): lax.psum_scatter(tap_terms, 'ctx', scatter_dimension=0, tiled=True)  63.3 us
    psum x1, waiting for transfers between devices, local(): tap_grad = lax.psum(segment, 'rep')  30.5 us
    all_gather x1, waiting for transfers between devices, local(): taps = lax.all_gather(filter_taps, 'ctx', axis=0, tiled=True)  29.1 us
    pallas_call x1, Pallas kernels, convolve(): pl.pallas_call(kernel, grid=(channels // TILE,), out_shape=(jax.ShapeDtyp...  13.8 us
    unnamed x13, local copies, waits for them, and re-layouts  7.56 us
  transfers between devices with their start and end apart: 5, of which 4 were waited for; matrix products, arithmetic and copies ran while one was open for 1% of the time, Pallas kernels for 0%

profile of v1, /device:TPU:0, one launch (start us, length us, event | category | flops | bytes accessed | tf_op | source)
XLA Modules:
  0.0 166.7 jit_solution(3052599468339675204)
XLA Ops:
  7.2 0.0 copy-start
  7.2 0.0 all-gather.2.cloned.1.call-start
  7.2 0.7 all-gather.2.cloned.1.call-update
  7.9 0.0 reduce-scatter.2.cloned.1.call-start
  8.6 1.3 bitcast_select_fusion
  10.0 1.3 collective-permute-start.1
  11.3 3.1 %collective-permute-start = (bf16[128,2048]{1,0:T(8,128)(2,1)S(1)}, bf16[128,2048]{1,0:T(8,128)(2,1)S(1)}, u32[]{:S(2)}, u32[]{:S(2)}) collective-permute-start(bf16[128,2048]{1,0:T(8,128)(2,1)S(1)} %get-tuple-element.7), channel_id=1, source_target_pairs={{0,8},{8,16},{16,24},{24,32},{32,40},{40,48},{48,56},{56,64},{64,7... | collective-permute-start | bytes 1572872 | tf_op jit(solution)/shard_map/ppermute | solution.py:135
  14.3 0.0 collective-permute-done.1.right_ref
  14.4 1.5 collective-permute-done.left_ref
  15.8 29.1 %all-gather.2.cloned.1.call-done.w_ref = bf16[256,2048]{1,0:T(8,128)(2,1)} async-done(((bf16[16,2048]{1,0:T(8,128)(2,1)}), bf16[256,2048]{1,0:T(8,128)(2,1)}) %all-gather.2.cloned.1.call-update) | async-done | bytes 1048592 | tf_op jit(solution)/shard_map/all_gather | solution.py:137
  44.9 0.0 copy-done
  44.9 0.0 copy-start.1
  44.9 1.6 copy-done.1
  46.5 0.0 copy-start.3
  46.5 1.2 copy-done.3
  47.7 0.0 copy-start.4
  47.7 0.9 copy-done.4
  48.6 0.0 copy-start.5
  48.6 0.9 copy-done.5
  49.6 13.8 %shard_map.77 = (bf16[512,2048]{1,0:T(8,128)(2,1)}, f32[256,2048]{1,0:T(8,128)S(1)}) custom-call(s32[1,1]{1,0:T(1,128)} %copy.9.count_ref, bf16[256,256]{1,0:T(8,128)(2,1)S(1)} %copy-done.5, bf16[128,768]{1,0:T(8,128)(2,1)S(1)} %copy-done.4, bf16[512,2048]{1,0:T(8,128)(2,1)S(1)} %bitcast.10, bf16[512,2048]{1,0:T(8,128)(2,1)S(1)} %bitcast.9, ...), custom_call_target="tpu_custom_call" | custom-call | tf_op jit(solution)/shard_map/pallas_call | solution.py:109
  63.3 0.0 copy-start.2
  63.3 1.3 copy-done.2
  64.7 0.0 reduce-scatter.2.cloned.1.call-update
  64.7 0.0 all-reduce.2.cloned.1.call-start
  64.7 63.3 %reduce-scatter.2.cloned.1.call-done = f32[16,2048]{1,0:T(8,128)} async-done(((f32[256,2048]{1,0:T(8,128)}), f32[16,2048]{1,0:T(8,128)}) %reduce-scatter.2.cloned.1.call-update) | async-done | bytes 131088 | tf_op jit(solution)/shard_map/reduce_scatter | solution.py:139
  128.1 0.0 all-reduce.2.cloned.1.call-update
  128.1 30.5 %all-reduce.2.cloned.1.call-done = f32[16,2048]{1,0:T(8,128)} async-done(((f32[16,2048]{1,0:T(8,128)}), f32[16,2048]{1,0:T(8,128)}) %all-reduce.2.cloned.1.call-update) | async-done | bytes 131088 | tf_op jit(solution)/shard_map/psum | solution.py:140
  158.6 1.6 copy.10
  (2 shorter events, 0.0 us)
Async XLA Ops:
  7.2 37.7 %copy-start = (bf16[1,512,2048]{2,1,0:T(8,128)(2,1)S(1)}, bf16[1,512,2048]{2,1,0:T(8,128)(2,1)}, u32[]{:S(2)}) copy-start(bf16[1,512,2048]{2,1,0:T(8,128)(2,1)} %param.7) | copy-start | bytes 6291460
  7.2 37.7 %all-gather.2.cloned.1.call-start = ((), (), s32[]{:S(2)}) async-start(), calls=%async_computation.1 | async-start | bytes 1114112 | tf_op jit(solution)/shard_map/all_gather | solution.py:137
  7.9 120.2 %reduce-scatter.2.cloned.1.call-start = ((), (), s32[]{:S(2)}) async-start(), calls=%async_computation.2 | async-start | bytes 2228224 | tf_op jit(solution)/shard_map/reduce_scatter | solution.py:139
  10.0 4.4 %collective-permute-start.1 = (bf16[128,2048]{1,0:T(8,128)(2,1)S(1)}, bf16[128,2048]{1,0:T(8,128)(2,1)S(1)}, u32[]{:S(2)}, u32[]{:S(2)}) collective-permute-start(bf16[128,2048]{1,0:T(8,128)(2,1)S(1)} %get-tuple-element.6), channel_id=1, source_target_pairs={{8,0},{16,8},{24,16},{32,24},{40,32},{48,40},{56,48},{64,56},{72,6... | collective-permute-start | bytes 1572872 | tf_op jit(solution)/shard_map/ppermute | solution.py:136
  11.3 4.6 %collective-permute-start = (bf16[128,2048]{1,0:T(8,128)(2,1)S(1)}, bf16[128,2048]{1,0:T(8,128)(2,1)S(1)}, u32[]{:S(2)}, u32[]{:S(2)}) collective-permute-start(bf16[128,2048]{1,0:T(8,128)(2,1)S(1)} %get-tuple-element.7), channel_id=1, source_target_pairs={{0,8},{8,16},{16,24},{24,32},{32,40},{40,48},{48,56},{56,64},{64,7... | collective-permute-start | bytes 1572872 | tf_op jit(solution)/shard_map/ppermute | solution.py:135
  44.9 1.6 copy-start.1
  46.5 1.2 copy-start.3
  47.7 0.9 copy-start.4
  48.6 0.9 copy-start.5
  63.3 1.3 copy-start.2
  64.7 93.9 %all-reduce.2.cloned.1.call-start = ((), (), s32[]{:S(2)}) async-start(), calls=%async_computation.3 | async-start | bytes 262144 | tf_op jit(solution)/shard_map/psum | solution.py:140
Sparse Core Ops, SparseCore 0:
  9.7 35.1 all-gather.1
  64.8 63.2 reduce-scatter.1
  130.5 28.0 all-reduce.1

commit v2 on v0

v2 whole, which is shorter than its diff:
```python
import functools
import math

import jax
import jax.numpy as jnp
import numpy as np
from jax import lax
from jax.experimental import pallas as pl
from jax.experimental.pallas import tpu as pltpu
from jax.sharding import PartitionSpec as P

REACH = 128
TILE = 256
STEP = 16
Z = 4


def transform_tables():
    freq = 2 * np.arange(128)[:, None] + 1
    analysis, synthesis = [], []
    for b in range(4):
        angle = np.pi * (freq * (np.arange(128)[None, :] + 128 * b) % 512) / 256.0
        forward = np.concatenate([np.cos(angle), -np.sin(angle)], 0)
        high = forward.astype(jnp.bfloat16)
        low = (forward - high.astype(np.float64)).astype(jnp.bfloat16)
        analysis.append(np.concatenate([high, low], 1))
        back = [part.astype(np.float64).T / 128 for part in (high, high, low)]
        synthesis.append(np.concatenate(back, 1))
    rows = [32 * z + 16 * core + 8 * half + r
            for core in range(2) for half in range(2) for z in range(Z) for r in range(8)]
    tap_scale = 1.0 / 128
    taps = [synthesis[h][rows] * tap_scale for h in range(2)]
    return (np.stack(analysis), np.stack(synthesis).astype(jnp.bfloat16),
            np.stack(taps).astype(jnp.bfloat16))


def split(value):
    high = value.astype(jnp.bfloat16)
    low = (value - high.astype(jnp.float32)).astype(jnp.bfloat16)
    return high, low


def kernel(tiles, count_ref, ana_ref, syn_ref, tsyn_ref, x_hbm, g_hbm, w_hbm,
           out_hbm, tap_hbm,
           gbuf, xbuf, obuf, from_left, from_right, wbuf,
           af, xf, gf, wf, yf, tf, tap, pair_in, xa_in, xb_in, z_in, fin,
           load_sem, out_sem, halo_s, halo_r, wz_s, wz_r, wx_s, wx_r, wp_s, wp_r,
           p_s, p_r, xa_s, xa_r, xb_s, xb_r, z_s, z_r, h_s, h_r):
    live_count = count_ref[0, 0]
    ctx = lax.axis_index("ctx")
    rep = lax.axis_index("rep")
    ends = 16
    core = lax.rem(ctx, 2)
    z = lax.rem(lax.div(ctx, 2), Z)
    xlo = lax.div(ctx, 8)
    half_cols = tiles * TILE // 2

    def device(x_lo, z_at, core_at, rep_at):
        return {"ctx": x_lo * 8 + z_at * 2 + core_at, "rep": rep_at}

    def remote(src, dst, send, recv, target):
        return pltpu.make_async_remote_copy(
            src_ref=src, dst_ref=dst, send_sem=send, recv_sem=recv,
            device_id=target, device_id_type=pl.DeviceIdType.MESH)

    left = {"ctx": lax.rem(ctx + ends - 1, ends), "rep": rep}
    right = {"ctx": lax.rem(ctx + 1, ends), "rep": rep}
    sibling = device(xlo, z, 1 - core, rep)
    x_near = device(1 - xlo, z, core, rep)
    x_wrap = device(1 - xlo, z, core, 1 - rep)
    x_far = device(xlo, z, core, 1 - rep)
    z_peers = [device(xlo, lax.rem(z + d, Z), core, rep) for d in range(1, Z)]

    barrier = pltpu.get_barrier_semaphore()
    peers = [left, right, x_near, x_wrap, x_far] + z_peers
    for peer in peers:
        pl.semaphore_signal(barrier, inc=1, device_id=peer, device_id_type=pl.DeviceIdType.MESH)

    own_half = pl.ds(pl.multiple_of(rep * half_cols, TILE // 2), half_cols)
    loads = [
        pltpu.make_async_copy(g_hbm.at[0, pl.ds(384, 128), :], gbuf.at[pl.ds(384, 128), :], load_sem.at[0]),
        pltpu.make_async_copy(w_hbm.at[:, own_half], wbuf.at[xlo, z, core, :, own_half], load_sem.at[1]),
        pltpu.make_async_copy(g_hbm.at[0, pl.ds(0, 384), :], gbuf.at[pl.ds(0, 384), :], load_sem.at[2]),
        pltpu.make_async_copy(x_hbm.at[0], xbuf, load_sem.at[3]),
    ]
    for copy in loads:
        copy.start()

    def cols(i):
        return pl.ds(pl.multiple_of(i * TILE, TILE), TILE)

    def live_rows(b):
        rows = lax.broadcasted_iota(jnp.int32, (REACH, TILE), 0) + b * REACH
        return rows < live_count

    def halo_right(i):
        return remote(gbuf.at[pl.ds(384, 128), cols(i)], from_left.at[i],
                      halo_s.at[0, i], halo_r.at[0, i], right)

    def halo_left(i):
        return remote(g_hbm.at[0, pl.ds(0, 128), cols(i)], from_right.at[i],
                      halo_s.at[1, i], halo_r.at[1, i], left)

    def taps_z(d):
        return remote(w_hbm.at[:, own_half], wbuf.at[xlo, z, core, :, own_half],
                      wz_s.at[d], wz_r.at[d], z_peers[d])

    def taps_z_arrival(d):
        source = lax.rem(z + Z - 1 - d, Z)
        return remote(w_hbm.at[:, own_half], wbuf.at[xlo, source, core, :, own_half],
                      wz_s.at[d], wz_r.at[d], z_peers[d])

    def taps_x(d):
        part = wbuf.at[xlo, :, core, :, own_half]
        return remote(part, part, wx_s.at[d], wx_r.at[d], (x_near, x_wrap, x_far)[d])

    def taps_x_arrival(d):
        other_half = pl.ds(pl.multiple_of((1 - rep) * half_cols, TILE // 2), half_cols)
        part = (wbuf.at[1 - xlo, :, core, :, own_half],
                wbuf.at[1 - xlo, :, core, :, other_half],
                wbuf.at[xlo, :, core, :, other_half])[d]
        return remote(part, part, wx_s.at[d], wx_r.at[d], (x_near, x_wrap, x_far)[d])

    def taps_pair(which):
        part = wbuf.at[:, :, which]
        return remote(part, part, wp_s, wp_r, sibling)

    def odd(i):
        return lax.rem(i, 2)

    def keep(i):
        return lax.rem(rep + (1 - odd(i)) * xlo, 2)

    def first_x(i):
        return device(1 - xlo, z, core, lax.rem(rep + odd(i), 2))

    def second_x(i):
        return device(1 - xlo, z, core, lax.rem(rep + 1 - odd(i), 2))

    def pair_copy(i):
        return remote(tap.at[i, 1 - core], pair_in.at[i], p_s.at[i], p_r.at[i], sibling)

    def xa_copy(i):
        return remote(tap.at[i, core, 1 - keep(i)], xa_in.at[i], xa_s.at[i], xa_r.at[i], first_x(i))

    def xb_copy(i):
        return remote(tap.at[i, core, keep(i), 1 - xlo], xb_in.at[i], xb_s.at[i], xb_r.at[i], second_x(i))

    def z_copy(i, d):
        rows = pl.ds(pl.multiple_of(lax.rem(z + 1 + d, Z) * 8, 8), 8)
        return remote(tap.at[i, core, keep(i), xlo, rows, :], z_in.at[i, d],
                      z_s.at[i, d], z_r.at[i, d], z_peers[d])

    def rep_copy(i, which):
        part = fin.at[pl.ds(pl.multiple_of(which * 8, 8), 8), cols(i)]
        return remote(part, part, h_s.at[i], h_r.at[i], x_far)

    def stage_pair(i):
        pair_copy(i).wait_recv()
        tap[i, core] += pair_in[i]
        xa_copy(i).start()

    def stage_xa(i):
        xa_copy(i).wait_recv()
        tap[i, core, keep(i)] += xa_in[i]
        xb_copy(i).start()

    def stage_xb(i):
        xb_copy(i).wait_recv()
        tap[i, core, keep(i), xlo] += xb_in[i]
        for d in range(Z - 1):
            z_copy(i, d).start()

    def stage_z(i):
        for d in range(Z - 1):
            z_copy(i, d).wait_recv()
        mine = tap[i, core, keep(i), xlo, pl.ds(pl.multiple_of(z * 8, 8), 8), :]
        total = (mine + z_in[i, 0]) + (z_in[i, 1] + z_in[i, 2])
        fin[pl.ds(pl.multiple_of(keep(i) * 8, 8), 8), cols(i)] = total
        rep_copy(i, keep(i)).start()

    def reduction(slot):
        for stage, lag in ((stage_z, 7), (stage_xb, 5), (stage_xa, 3), (stage_pair, 1)):
            i = slot - lag

            @pl.when(jnp.logical_and(i >= 0, i < tiles))
            def _(stage=stage, i=i):
                stage(i)

    loads[0].wait()
    tail_live = live_rows(3)

    def mask_tail(i, carry):
        gbuf[pl.ds(384, 128), cols(i)] = jnp.where(tail_live, gbuf[pl.ds(384, 128), cols(i)], 0)
        return carry

    lax.fori_loop(0, tiles, mask_tail, None)
    pl.semaphore_wait(barrier, len(peers))

    def send_halo(i, carry):
        @pl.when(ctx < ends - 1)
        def _():
            halo_right(i).start()

        @pl.when(ctx > 0)
        def _():
            halo_left(i).start()

        return carry

    send_halo(0, None)
    for d in range(Z - 1):
        taps_z(d).start()
    lax.fori_loop(1, tiles, send_halo, None)

    @pl.when(ctx == 0)
    def _():
        from_left[...] = jnp.zeros_like(from_left)

    @pl.when(ctx == ends - 1)
    def _():
        from_right[...] = jnp.zeros_like(from_right)

    for copy in loads[2:]:
        copy.wait()

    def analyse(b, block):
        return jnp.dot(ana_ref[b % 4], jnp.concatenate([block, block], 0),
                       preferred_element_type=jnp.float32)

    def put(ref, at, row, value):
        high, low = split(value)
        ref[at, pl.ds(row, STEP), :] = high
        ref[at, pl.ds(256 + row, STEP), :] = low
        ref[at, pl.ds(512 + row, STEP), :] = high

    def tap_tile(i, carry):
        for b in range(4):
            rows = pl.ds(b * REACH, REACH)
            g_block, x_block = gbuf[rows, cols(i)], xbuf[rows, cols(i)]
            if b > 0:
                x_block = jnp.where(live_rows(b), x_block, 0)
            if b in (1, 2):
                g_block = jnp.where(live_rows(b), g_block, 0)
            af[b + 1] = analyse(b + 1, g_block)
            xf[b] = analyse(b, x_block)

        @pl.when(ctx > 0)
        def _():
            halo_right(i).wait_recv()

        @pl.when(ctx < ends - 1)
        def _():
            halo_left(i).wait_recv()

        af[0] = analyse(0, from_left[i])
        af[5] = analyse(5, from_right[i])

        def chunk(c, carry):
            row = pl.multiple_of(c * STEP, STEP)
            re, im = pl.ds(row, STEP), pl.ds(128 + row, STEP)
            ar = [af[b, re, :] for b in range(6)]
            ai = [af[b, im, :] for b in range(6)]
            gr = [ar[b] + ar[b + 1] for b in range(5)]
            gi = [ai[b] + ai[b + 1] for b in range(5)]
            for b in range(5):
                gf[i, b, re, :] = gr[b]
                gf[i, b, im, :] = gi[b]
            for h in range(2):
                tr = ti = None
                for b in range(4):
                    xr, xi = xf[b, re, :], xf[b, im, :]
                    pr = xr * gr[b + h] + xi * gi[b + h]
                    pi = xr * gi[b + h] - xi * gr[b + h]
                    tr, ti = (pr, pi) if tr is None else (tr + pr, ti + pi)
                put(tf, h, row, tr)
                put(tf, h, 128 + row, ti)
            return carry

        lax.fori_loop(0, 128 // STEP, chunk, None)
        for h in range(2):
            terms = jnp.dot(tsyn_ref[h], tf[h], preferred_element_type=jnp.float32)
            for core_at in range(2):
                for half in range(2):
                    start = (core_at * 2 + half) * 32
                    tap[i, core_at, half, h] = terms[start:start + 32]
        pair_copy(i).start()
        reduction(i)

        @pl.when(i == 0)
        def _():
            loads[1].wait()
            for d in range(Z - 1):
                taps_z_arrival(d).wait_recv()
            for d in range(3):
                taps_x(d).start()

        @pl.when(i == tiles - 2)
        def _():
            for d in range(3):
                taps_x_arrival(d).wait_recv()
            taps_pair(core).start()

        return carry

    lax.fori_loop(0, tiles, tap_tile, None)
    taps_pair(1 - core).wait_recv()

    def store_out(i):
        return pltpu.make_async_copy(obuf.at[:, cols(i)], out_hbm.at[0, :, cols(i)], out_sem.at[i])

    def grad_tile(i, carry):
        for h in range(2):
            block = wbuf[h, :, :, :, cols(i)].reshape(REACH, TILE)
            wf[h] = analyse(h, block)

        def chunk(c, carry):
            row = pl.multiple_of(c * STEP, STEP)
            re, im = pl.ds(row, STEP), pl.ds(128 + row, STEP)
            gr = [gf[i, b, re, :] for b in range(5)]
            gi = [gf[i, b, im, :] for b in range(5)]
            w0r, w0i = wf[0, re, :], wf[0, im, :]
            w1r, w1i = wf[1, re, :], wf[1, im, :]
            for b in range(4):
                yr = (w0r * gr[b] + w0i * gi[b]) + (w1r * gr[b + 1] + w1i * gi[b + 1])
                yi = (w0r * gi[b] - w0i * gr[b]) + (w1r * gi[b + 1] - w1i * gr[b + 1])
                put(yf, b, row, yr)
                put(yf, b, 128 + row, yi)
            return carry

        lax.fori_loop(0, 128 // STEP, chunk, None)
        for b in range(4):
            value = jnp.dot(syn_ref[b], yf[b], preferred_element_type=jnp.float32)
            if b > 0:
                value = jnp.where(live_rows(b), value, 0)
            obuf[pl.ds(b * REACH, REACH), cols(i)] = value.astype(jnp.bfloat16)
        store_out(i).start()
        reduction(i + tiles)
        return carry

    lax.fori_loop(0, tiles, grad_tile, None)
    for slot in range(2 * tiles, tiles + 7):
        reduction(slot)

    def finish(i, carry):
        rep_copy(i, 1 - keep(i)).wait_recv()
        rep_copy(i, keep(i)).wait_send()
        store_out(i).wait()
        pair_copy(i).wait_send()
        xa_copy(i).wait_send()
        xb_copy(i).wait_send()
        for d in range(Z - 1):
            z_copy(i, d).wait_send()

        @pl.when(ctx < ends - 1)
        def _():
            halo_right(i).wait_send()

        @pl.when(ctx > 0)
        def _():
            halo_left(i).wait_send()

        return carry

    lax.fori_loop(0, tiles, finish, None)
    last = pltpu.make_async_copy(fin, tap_hbm, load_sem.at[4])
    last.start()
    for d in range(3):
        taps_z(d).wait_send()
        taps_x(d).wait_send()
    taps_pair(core).wait_send()
    last.wait()


def fused(counts, x, g, taps):
    _, rows, channels = x.shape
    tiles = channels // TILE
    ana, syn, tsyn = transform_tables()
    dma = pltpu.SemaphoreType.DMA
    vmem = pl.BlockSpec(memory_space=pltpu.VMEM)
    hbm = pl.BlockSpec(memory_space=pl.ANY)
    f32, bf16 = jnp.float32, jnp.bfloat16
    return pl.pallas_call(
        functools.partial(kernel, tiles),
        out_shape=(jax.ShapeDtypeStruct(x.shape, bf16),
                   jax.ShapeDtypeStruct(taps.shape, f32)),
        in_specs=[pl.BlockSpec(memory_space=pltpu.SMEM), vmem, vmem, vmem, hbm, hbm, hbm],
        out_specs=(hbm, hbm),
        scratch_shapes=[
            pltpu.VMEM((rows, channels), bf16),
            pltpu.VMEM((rows, channels), bf16),
            pltpu.VMEM((rows, channels), bf16),
            pltpu.VMEM((tiles, REACH, TILE), bf16),
            pltpu.VMEM((tiles, REACH, TILE), bf16),
            pltpu.VMEM((2, Z, 2, 16, channels), bf16),
            pltpu.VMEM((6, 256, TILE), f32),
            pltpu.VMEM((4, 256, TILE), f32),
            pltpu.VMEM((tiles, 5, 256, TILE), f32),
            pltpu.VMEM((2, 256, TILE), f32),
            pltpu.VMEM((4, 768, TILE), bf16),
            pltpu.VMEM((2, 768, TILE), bf16),
            pltpu.VMEM((tiles, 2, 2, 2, 32, TILE), f32),
            pltpu.VMEM((tiles, 2, 2, 32, TILE), f32),
            pltpu.VMEM((tiles, 2, 32, TILE), f32),
            pltpu.VMEM((tiles, 32, TILE), f32),
            pltpu.VMEM((tiles, Z - 1, 8, TILE), f32),
            pltpu.VMEM((16, channels), f32),
            dma((5,)), dma((tiles,)),
            dma((2, tiles)), dma((2, tiles)),
            dma((3,)), dma((3,)), dma((3,)), dma((3,)), dma, dma,
            dma((tiles,)), dma((tiles,)),
            dma((tiles,)), dma((tiles,)),
            dma((tiles,)), dma((tiles,)),
            dma((tiles, 3)), dma((tiles, 3)),
            dma((tiles,)), dma((tiles,)),
        ],
        compiler_params=pltpu.CompilerParams(
            collective_id=0, has_side_effects=True, vmem_limit_bytes=56 << 20),
    )(counts, jnp.asarray(ana), jnp.asarray(syn), jnp.asarray(tsyn), x, g, taps)


def local(saved_input, out_grad, filter_taps, valid_counts):
    return fused(valid_counts, saved_input, out_grad, filter_taps)


def solution(mesh):
    return jax.shard_map(
        local,
        mesh=mesh,
        in_specs=(P("rep", "ctx", "ch"), P("rep", "ctx", "ch"), P("ctx", "ch"), P("rep", "ctx")),
        out_specs=(P("rep", "ctx", "ch"), P("ctx", "ch")),
        check_vma=False,
    )
```

time: 1260 us -> 55.2 us (0.04); the launches traced: 1240 us -> 55 us
  local copies, waits for them, and re-layouts: 1030 us -> 3.85 us
  matrix products: 124 us -> 0 us
  Pallas kernels: 0 us -> 49.9 us
  waiting for transfers between devices: 41 us -> 0 us
  other arithmetic: 19.4 us -> 0 us
  between operations: 14.5 us -> 1.29 us
    another operation x512 -> x0, local copies, waits for them, and re-layouts: 587 us -> none  [the longest x448 417 us: one_group(): jnp.stack([signal_part[row_block * offset:row_block * offset + window] fo...]
    reshape x32 -> x0, local copies, waits for them, and re-layouts: 204 us -> none  [one_group(): toeplitz = flattened.reshape(row_block, window, lane_width)]
    slice x33 -> x0, local copies, waits for them, and re-layouts: 130 us -> none  [the longest x32 129 us: one_group(): flattened = jnp.tile(extended, (row_block, 1))[:row_block * window]]
    dot_general x32 -> x0, matrix products: 124 us -> none  [one_group(): jnp.einsum('bjc,ajc->abc', toeplitz, windows, preferred_element_type=jnp....]
    pallas_call x0 -> x1, Pallas kernels: none -> 49.9 us  [fused(): pl.pallas_call(functools.partial(kernel, tiles), out_shape=(jax.ShapeDtyp...]
    psum x1 -> x0, waiting for transfers between devices: 40.9 us -> none  [local(): tap_grad = lax.psum(segment, 'rep')]
    transpose x32 -> x0, local copies, waits for them, and re-layouts: 29.1 us -> none  [one_group(): jnp.einsum('bjc,ajc->abc', toeplitz, windows, preferred_element_type=jnp....]
    dynamic_slice x32 -> x0, local copies, waits for them, and re-layouts: 28.2 us -> none  [one_group(): tap_part = lax.dynamic_slice_in_dim(taps, column, lane_width, 1)]
  transfers between devices with their start and end apart: 5 -> 0, of which waited for: 1 -> 0; matrix products, arithmetic and copies ran while one was open for 94% -> 0% of each run, Pallas kernels for 0% -> 0%
where the time goes in v2:
time: 55.2 us; the launch traced here: 55 us
  Pallas kernels  49.9 us (90%)
  local copies, waits for them, and re-layouts  3.85 us (7%)
  between operations  1.29 us (2%)
    pallas_call x1, Pallas kernels, fused(): pl.pallas_call(functools.partial(kernel, tiles), out_shape=(jax.ShapeDtyp...  49.9 us
    unnamed x4, local copies, waits for them, and re-layouts  3.85 us

profile of v2, /device:TPU:0, one launch (start us, length us, event | category | flops | bytes accessed | tf_op | source)
XLA Modules:
  0.0 55.0 jit_solution(2304275155130813773)
XLA Ops:
  1.3 49.9 %shard_map.86 = (bf16[1,512,2048]{2,1,0:T(8,128)(2,1)}, f32[16,2048]{1,0:T(8,128)}) custom-call(s32[1,1]{1,0:T(1,128)S(6)} %copy.11.count_ref, bf16[4,256,256]{2,1,0:T(8,128)(2,1)} %constant.6.clone.ana_ref, bf16[4,128,768]{2,1,0:T(8,128)(2,1)} %constant.7.clone.syn_ref, bf16[2,128,768]{2,1,0:T(8,128)(2,1)} %constant.8.clone.tsyn_ref, ...), custom_call_target="tpu_custom_call" | custom-call | tf_op jit(solution)/shard_map/pallas_call | solution.py:383
  51.1 0.0 copy-start
  51.2 3.2 %copy.12 = bf16[1,512,2048]{2,1,0:T(8,128)(2,1)} copy(bf16[1,512,2048]{2,1,0:T(8,128)(2,1)} %get-tuple-element.4) | data formatting | bytes 4194304
  54.4 0.0 copy-done
  54.4 0.7 %copy.13 = f32[16,2048]{1,0:T(8,128)} copy(f32[16,2048]{1,0:T(8,128)S(1)} %copy-done) | data formatting | bytes 262144
Async XLA Ops:
  51.1 3.2 %copy-start = (f32[16,2048]{1,0:T(8,128)S(1)}, f32[16,2048]{1,0:T(8,128)}, u32[]{:S(2)}) copy-start(f32[16,2048]{1,0:T(8,128)} %get-tuple-element.5) | copy-start | bytes 393220

commit v3 on v2

v3 whole, which is shorter than its diff:
```python
import functools
import math

import jax
import jax.numpy as jnp
import numpy as np
from jax import lax
from jax.experimental import pallas as pl
from jax.experimental.pallas import tpu as pltpu
from jax.sharding import PartitionSpec as P

REACH = 128
TILE = 256
STEP = 16
Z = 4


def transform_tables():
    freq = 2 * np.arange(128)[:, None] + 1
    analysis, synthesis = [], []
    for b in range(4):
        angle = np.pi * (freq * (np.arange(128)[None, :] + 128 * b) % 512) / 256.0
        forward = np.concatenate([np.cos(angle), -np.sin(angle)], 0)
        high = forward.astype(jnp.bfloat16)
        low = (forward - high.astype(np.float64)).astype(jnp.bfloat16)
        analysis.append(np.concatenate([high, low], 1))
        back = [part.astype(np.float64).T / 128 for part in (high, high, low)]
        synthesis.append(np.concatenate(back, 1))
    rows = [32 * z + 16 * core + r for core in range(2) for z in range(Z) for r in range(16)]
    tap_scale = 1.0 / 128
    taps = [synthesis[h][rows] * tap_scale for h in range(2)]
    return (np.stack(analysis), np.stack(synthesis).astype(jnp.bfloat16),
            np.stack(taps).astype(jnp.bfloat16))


def split(value):
    high = value.astype(jnp.bfloat16)
    low = (value - high.astype(jnp.float32)).astype(jnp.bfloat16)
    return high, low


def kernel(tiles, count_ref, ana_hbm, syn_hbm, tsyn_hbm, x_hbm, g_hbm, w_hbm,
           out_hbm, tap_hbm,
           ana_ref, syn_ref, tsyn_ref, gbuf, xbuf, obuf, from_left, from_right, wbuf,
           af, xf, wf, yf, tf, tap, pair_in, z_in, x_in, fin,
           load_sem, out_sem, halo_s, halo_r, wz_s, wz_r, wx_s, wx_r, wp_s, wp_r,
           p_s, p_r, z_s, z_r, x_s, x_r):
    live_count = count_ref[0, 0]
    ctx = lax.axis_index("ctx")
    rep = lax.axis_index("rep")
    ends = 16
    core = lax.rem(ctx, 2)
    z = lax.rem(lax.div(ctx, 2), Z)
    xlo = lax.div(ctx, 8)
    chunks = tiles // 2
    half_cols = chunks * TILE

    def device(x_lo, z_at, core_at, rep_at):
        return {"ctx": x_lo * 8 + z_at * 2 + core_at, "rep": rep_at}

    def remote(src, dst, send, recv, target):
        return pltpu.make_async_remote_copy(
            src_ref=src, dst_ref=dst, send_sem=send, recv_sem=recv,
            device_id=target, device_id_type=pl.DeviceIdType.MESH)

    left = {"ctx": lax.rem(ctx + ends - 1, ends), "rep": rep}
    right = {"ctx": lax.rem(ctx + 1, ends), "rep": rep}
    sibling = device(xlo, z, 1 - core, rep)
    x_near = device(1 - xlo, z, core, rep)
    x_wrap = device(1 - xlo, z, core, 1 - rep)
    x_far = device(xlo, z, core, 1 - rep)
    x_peers = (x_near, x_wrap, x_far)
    z_peers = [device(xlo, lax.rem(z + d, Z), core, rep) for d in range(1, Z)]

    barrier = pltpu.get_barrier_semaphore()
    peers = [left, right, x_near, x_wrap, x_far] + z_peers
    for peer in peers:
        pl.semaphore_signal(barrier, inc=1, device_id=peer, device_id_type=pl.DeviceIdType.MESH)

    own_half = pl.ds(pl.multiple_of(rep * half_cols, TILE // 2), half_cols)
    loads = [
        pltpu.make_async_copy(g_hbm.at[0, pl.ds(384, 128), :], gbuf.at[pl.ds(384, 128), :], load_sem.at[0]),
        pltpu.make_async_copy(w_hbm.at[:, own_half], wbuf.at[xlo, z, core, :, own_half], load_sem.at[1]),
        pltpu.make_async_copy(g_hbm.at[0, pl.ds(0, 384), :], gbuf.at[pl.ds(0, 384), :], load_sem.at[2]),
        pltpu.make_async_copy(x_hbm.at[0], xbuf, load_sem.at[3]),
        pltpu.make_async_copy(ana_hbm, ana_ref, load_sem.at[4]),
        pltpu.make_async_copy(tsyn_hbm, tsyn_ref, load_sem.at[5]),
        pltpu.make_async_copy(syn_hbm, syn_ref, load_sem.at[6]),
    ]
    for copy in loads:
        copy.start()

    def cols(i):
        return pl.ds(pl.multiple_of(i * TILE, TILE), TILE)

    def live_rows(b):
        rows = lax.broadcasted_iota(jnp.int32, (REACH, TILE), 0) + b * REACH
        return rows < live_count

    def halo_right(i):
        return remote(gbuf.at[pl.ds(384, 128), cols(i)], from_left.at[i],
                      halo_s.at[0, i], halo_r.at[0, i], right)

    def halo_left(i):
        return remote(g_hbm.at[0, pl.ds(0, 128), cols(i)], from_right.at[i],
                      halo_s.at[1, i], halo_r.at[1, i], left)

    def taps_z(d):
        return remote(w_hbm.at[:, own_half], wbuf.at[xlo, z, core, :, own_half],
                      wz_s.at[d], wz_r.at[d], z_peers[d])

    def taps_z_arrival(d):
        source = lax.rem(z + Z - 1 - d, Z)
        return remote(w_hbm.at[:, own_half], wbuf.at[xlo, source, core, :, own_half],
                      wz_s.at[d], wz_r.at[d], z_peers[d])

    def half_tile(half, c):
        return pl.ds(pl.multiple_of((half * chunks + c) * TILE, TILE), TILE)

    def taps_x(c, d):
        part = wbuf.at[xlo, :, core, :, half_tile(rep, c)]
        return remote(part, part, wx_s.at[c, d], wx_r.at[c, d], x_peers[d])

    def taps_x_arrival(c, d):
        x_from = (1 - xlo, 1 - xlo, xlo)[d]
        half_from = (rep, 1 - rep, 1 - rep)[d]
        part = wbuf.at[x_from, :, core, :, half_tile(half_from, c)]
        return remote(part, part, wx_s.at[c, d], wx_r.at[c, d], x_peers[d])

    def taps_pair(c, half, which):
        part = wbuf.at[:, :, which, :, half_tile(half, c)]
        return remote(part, part, wp_s.at[c, half], wp_r.at[c, half], sibling)

    def taps_forward(c):
        for d in range(3):
            taps_x_arrival(c, d).wait_recv()
        for half in range(2):
            taps_pair(c, half, core).start()

    def pair_copy(i):
        return remote(tap.at[i, 1 - core], pair_in.at[i], p_s.at[i], p_r.at[i], sibling)

    def z_copy(i, d):
        return remote(tap.at[i, core, lax.rem(z + 1 + d, Z)], z_in.at[i, d],
                      z_s.at[i, d], z_r.at[i, d], z_peers[d])

    def x_copy(i, d):
        h = (1 - xlo, 1 - xlo, xlo)[d]
        return remote(tap.at[i, core, z, h], x_in.at[i, d], x_s.at[i, d], x_r.at[i, d], x_peers[d])

    def stage_pair(i):
        pair_copy(i).wait_recv()
        tap[i, core] += pair_in[i]
        for d in range(Z - 1):
            z_copy(i, d).start()

    def stage_z(i):
        for d in range(Z - 1):
            z_copy(i, d).wait_recv()
        tap[i, core, z] = (tap[i, core, z] + z_in[i, 0]) + (z_in[i, 1] + z_in[i, 2])
        for d in range(3):
            x_copy(i, d).start()

    def stage_x(i):
        for d in range(3):
            x_copy(i, d).wait_recv()
        fin[:, cols(i)] = (tap[i, core, z, xlo] + x_in[i, 2]) + (x_in[i, 0] + x_in[i, 1])

    loads[0].wait()
    tail_live = live_rows(3)

    def mask_tail(i, carry):
        gbuf[pl.ds(384, 128), cols(i)] = jnp.where(tail_live, gbuf[pl.ds(384, 128), cols(i)], 0)
        return carry

    lax.fori_loop(0, tiles, mask_tail, None)
    pl.semaphore_wait(barrier, len(peers))

    def send_halo(i, carry):
        @pl.when(ctx < ends - 1)
        def _():
            halo_right(i).start()

        @pl.when(ctx > 0)
        def _():
            halo_left(i).start()

        return carry

    send_halo(0, None)
    for d in range(Z - 1):
        taps_z(d).start()
    lax.fori_loop(1, tiles, send_halo, None)

    @pl.when(ctx == 0)
    def _():
        from_left[...] = jnp.zeros_like(from_left)

    @pl.when(ctx == ends - 1)
    def _():
        from_right[...] = jnp.zeros_like(from_right)

    for copy in loads[2:5]:
        copy.wait()

    def analyse(b, block):
        return jnp.dot(ana_ref[b % 4], jnp.concatenate([block, block], 0),
                       preferred_element_type=jnp.float32)

    def put(ref, at, row, value):
        high, low = split(value)
        ref[at, pl.ds(row, STEP), :] = high
        ref[at, pl.ds(256 + row, STEP), :] = low
        ref[at, pl.ds(512 + row, STEP), :] = high

    def own_tile(i, carry):
        for b in range(4):
            rows = pl.ds(b * REACH, REACH)
            g_block, x_block = gbuf[rows, cols(i)], xbuf[rows, cols(i)]
            if b > 0:
                x_block = jnp.where(live_rows(b), x_block, 0)
            if b in (1, 2):
                g_block = jnp.where(live_rows(b), g_block, 0)
            af[i, b + 1] = analyse(b + 1, g_block)
            xf[i, b] = analyse(b, x_block)
        return carry

    lax.fori_loop(0, tiles, own_tile, None)
    loads[1].wait()
    for d in range(Z - 1):
        taps_z_arrival(d).wait_recv()
    for c in range(chunks):
        for d in range(3):
            taps_x(c, d).start()
    loads[5].wait()
    loads[6].wait()

    def windows(i, re, im):
        ar = [af[i, b, re, :] for b in range(6)]
        ai = [af[i, b, im, :] for b in range(6)]
        return [ar[b] + ar[b + 1] for b in range(5)], [ai[b] + ai[b + 1] for b in range(5)]

    def tap_tile(i, carry):
        @pl.when(ctx > 0)
        def _():
            halo_right(i).wait_recv()

        @pl.when(ctx < ends - 1)
        def _():
            halo_left(i).wait_recv()

        af[i, 0] = analyse(0, from_left[i])
        af[i, 5] = analyse(5, from_right[i])

        def chunk(c, carry):
            row = pl.multiple_of(c * STEP, STEP)
            re, im = pl.ds(row, STEP), pl.ds(128 + row, STEP)
            gr, gi = windows(i, re, im)
            for h in range(2):
                tr = ti = None
                for b in range(4):
                    xr, xi = xf[i, b, re, :], xf[i, b, im, :]
                    pr = xr * gr[b + h] + xi * gi[b + h]
                    pi = xr * gi[b + h] - xi * gr[b + h]
                    tr, ti = (pr, pi) if tr is None else (tr + pr, ti + pi)
                put(tf, h, row, tr)
                put(tf, h, 128 + row, ti)
            return carry

        lax.fori_loop(0, 128 // STEP, chunk, None, unroll=True)
        for h in range(2):
            terms = jnp.dot(tsyn_ref[h], tf[h], preferred_element_type=jnp.float32)
            for core_at in range(2):
                for z_at in range(Z):
                    start = (core_at * Z + z_at) * 16
                    tap[i, core_at, z_at, h] = terms[start:start + 16]
        pair_copy(i).start()

        @pl.when(i >= 1)
        def _():
            stage_pair(i - 1)

        for c in range(min(2, chunks)):
            @pl.when(i == tiles - 2 + c)
            def _(c=c):
                taps_forward(c)

        return carry

    lax.fori_loop(0, tiles, tap_tile, None)
    stage_pair(tiles - 1)

    def store_out(i):
        return pltpu.make_async_copy(obuf.at[:, cols(i)], out_hbm.at[0, :, cols(i)], out_sem.at[i])

    def grad_tile(k, carry):
        chunk_at = lax.div(k, 2)
        i = lax.rem(k, 2) * chunks + chunk_at

        @pl.when(lax.rem(k, 2) == 0)
        def _():
            for half in range(2):
                taps_pair(chunk_at, half, 1 - core).wait_recv()

        for h in range(2):
            block = wbuf[h, :, :, :, cols(i)].reshape(REACH, TILE)
            wf[h] = analyse(h, block)

        def chunk(c, carry):
            row = pl.multiple_of(c * STEP, STEP)
            re, im = pl.ds(row, STEP), pl.ds(128 + row, STEP)
            gr, gi = windows(i, re, im)
            w0r, w0i = wf[0, re, :], wf[0, im, :]
            w1r, w1i = wf[1, re, :], wf[1, im, :]
            for b in range(4):
                yr = (w0r * gr[b] + w0i * gi[b]) + (w1r * gr[b + 1] + w1i * gi[b + 1])
                yi = (w0r * gi[b] - w0i * gr[b]) + (w1r * gi[b + 1] - w1i * gr[b + 1])
                put(yf, b, row, yr)
                put(yf, b, 128 + row, yi)
            return carry

        lax.fori_loop(0, 128 // STEP, chunk, None, unroll=True)
        for b in range(4):
            value = jnp.dot(syn_ref[b], yf[b], preferred_element_type=jnp.float32)
            if b > 0:
                value = jnp.where(live_rows(b), value, 0)
            obuf[pl.ds(b * REACH, REACH), cols(i)] = value.astype(jnp.bfloat16)
        store_out(i).start()
        @pl.when(jnp.logical_and(lax.rem(k, 2) == 1, chunk_at + 2 < chunks))
        def _():
            taps_forward(chunk_at + 2)

        @pl.when(k >= 1)
        def _():
            stage_z(k - 1)

        return carry

    lax.fori_loop(0, tiles, grad_tile, None)
    stage_z(tiles - 1)

    def total(i, carry):
        stage_x(i)
        return carry

    lax.fori_loop(0, tiles, total, None)
    last = pltpu.make_async_copy(fin, tap_hbm, load_sem.at[7])
    last.start()

    def finish(i, carry):
        store_out(i).wait()
        pair_copy(i).wait_send()
        for d in range(3):
            z_copy(i, d).wait_send()
            x_copy(i, d).wait_send()

        @pl.when(ctx < ends - 1)
        def _():
            halo_right(i).wait_send()

        @pl.when(ctx > 0)
        def _():
            halo_left(i).wait_send()

        return carry

    lax.fori_loop(0, tiles, finish, None)
    for d in range(3):
        taps_z(d).wait_send()
    for c in range(chunks):
        for d in range(3):
            taps_x(c, d).wait_send()
        for half in range(2):
            taps_pair(c, half, core).wait_send()
    last.wait()


def fused(counts, x, g, taps):
    _, rows, channels = x.shape
    tiles = channels // TILE
    ana, syn, tsyn = transform_tables()
    dma = pltpu.SemaphoreType.DMA
    hbm = pl.BlockSpec(memory_space=pl.ANY)
    f32, bf16 = jnp.float32, jnp.bfloat16
    return pl.pallas_call(
        functools.partial(kernel, tiles),
        out_shape=(jax.ShapeDtypeStruct(x.shape, bf16),
                   jax.ShapeDtypeStruct(taps.shape, f32)),
        in_specs=[pl.BlockSpec(memory_space=pltpu.SMEM)] + [hbm] * 6,
        out_specs=(hbm, hbm),
        scratch_shapes=[
            pltpu.VMEM(ana.shape, bf16),
            pltpu.VMEM(syn.shape, bf16),
            pltpu.VMEM(tsyn.shape, bf16),
            pltpu.VMEM((rows, channels), bf16),
            pltpu.VMEM((rows, channels), bf16),
            pltpu.VMEM((rows, channels), bf16),
            pltpu.VMEM((tiles, REACH, TILE), bf16),
            pltpu.VMEM((tiles, REACH, TILE), bf16),
            pltpu.VMEM((2, Z, 2, 16, channels), bf16),
            pltpu.VMEM((tiles, 6, 256, TILE), f32),
            pltpu.VMEM((tiles, 4, 256, TILE), f32),
            pltpu.VMEM((2, 256, TILE), f32),
            pltpu.VMEM((4, 768, TILE), bf16),
            pltpu.VMEM((2, 768, TILE), bf16),
            pltpu.VMEM((tiles, 2, Z, 2, 16, TILE), f32),
            pltpu.VMEM((tiles, Z, 2, 16, TILE), f32),
            pltpu.VMEM((tiles, 3, 2, 16, TILE), f32),
            pltpu.VMEM((tiles, 3, 16, TILE), f32),
            pltpu.VMEM((16, channels), f32),
            dma((8,)), dma((tiles,)),
            dma((2, tiles)), dma((2, tiles)),
            dma((3,)), dma((3,)),
            dma((tiles // 2, 3)), dma((tiles // 2, 3)),
            dma((tiles // 2, 2)), dma((tiles // 2, 2)),
            dma((tiles,)), dma((tiles,)),
            dma((tiles, 3)), dma((tiles, 3)),
            dma((tiles, 3)), dma((tiles, 3)),
        ],
        compiler_params=pltpu.CompilerParams(
            collective_id=0, has_side_effects=True, vmem_limit_bytes=56 << 20),
    )(counts, jnp.asarray(ana), jnp.asarray(syn), jnp.asarray(tsyn), x, g, taps)


def local(saved_input, out_grad, filter_taps, valid_counts):
    return fused(valid_counts, saved_input, out_grad, filter_taps)


def solution(mesh):
    return jax.shard_map(
        local,
        mesh=mesh,
        in_specs=(P("rep", "ctx", "ch"), P("rep", "ctx", "ch"), P("ctx", "ch"), P("rep", "ctx")),
        out_specs=(P("rep", "ctx", "ch"), P("ctx", "ch")),
        check_vma=False,
    )
```

time: 55.2 us -> 41.9 us (0.76)
  Pallas kernels: 49.9 us -> 36.6 us
    pallas_call x1, Pallas kernels: 49.9 us -> 36.6 us  [fused(): pl.pallas_call(functools.partial(kernel, tiles), out_shape=(jax.ShapeDtyp...]
where the time goes in v3:
time: 41.9 us; the launch traced here: 41.7 us
  Pallas kernels  36.6 us (87%)
  local copies, waits for them, and re-layouts  3.85 us (9%)
  between operations  1.29 us (3%)
    pallas_call x1, Pallas kernels, fused(): pl.pallas_call(functools.partial(kernel, tiles), out_shape=(jax.ShapeDtyp...  36.6 us
    unnamed x4, local copies, waits for them, and re-layouts  3.85 us

profile of v3, /device:TPU:0, one launch (start us, length us, event | category | flops | bytes accessed | tf_op | source)
XLA Modules:
  0.0 41.7 jit_solution(16321968477484025853)
XLA Ops:
  1.3 36.6 %shard_map.86 = (bf16[1,512,2048]{2,1,0:T(8,128)(2,1)}, f32[16,2048]{1,0:T(8,128)}) custom-call(s32[1,1]{1,0:T(1,128)S(6)} %copy.11.count_ref, bf16[4,256,256]{2,1,0:T(8,128)(2,1)} %constant.6.clone.ana_hbm, bf16[4,128,768]{2,1,0:T(8,128)(2,1)} %constant.7.clone.syn_hbm, bf16[2,128,768]{2,1,0:T(8,128)(2,1)} %constant.8.clone.tsyn_hbm, ...), custom_call_target="tpu_custom_call" | custom-call | tf_op jit(solution)/shard_map/pallas_call | solution.py:385
  37.9 0.0 copy-start
  37.9 3.2 %copy.12 = bf16[1,512,2048]{2,1,0:T(8,128)(2,1)} copy(bf16[1,512,2048]{2,1,0:T(8,128)(2,1)} %get-tuple-element.4) | data formatting | bytes 4194304
  41.1 0.0 copy-done
  41.1 0.7 %copy.13 = f32[16,2048]{1,0:T(8,128)} copy(f32[16,2048]{1,0:T(8,128)S(1)} %copy-done) | data formatting | bytes 262144
Async XLA Ops:
  37.9 3.2 %copy-start = (f32[16,2048]{1,0:T(8,128)S(1)}, f32[16,2048]{1,0:T(8,128)}, u32[]{:S(2)}) copy-start(f32[16,2048]{1,0:T(8,128)} %get-tuple-element.5) | copy-start | bytes 393220

commit v4 on v3

--- a/solution.py
+++ b/solution.py
@@ -26,11 +26,13 @@
         analysis.append(np.concatenate([high, low], 1))
         back = [part.astype(np.float64).T / 128 for part in (high, high, low)]
         synthesis.append(np.concatenate(back, 1))
-    rows = [32 * z + 16 * core + r for core in range(2) for z in range(Z) for r in range(16)]
+    x_rows = [32 * z + 16 * core + 8 * half + r
+              for core in range(2) for half in range(2) for z in range(Z) for r in range(8)]
+    z_rows = [32 * z + 16 * core + r for core in range(2) for z in range(Z) for r in range(16)]
     tap_scale = 1.0 / 128
-    taps = [synthesis[h][rows] * tap_scale for h in range(2)]
-    return (np.stack(analysis), np.stack(synthesis).astype(jnp.bfloat16),
-            np.stack(taps).astype(jnp.bfloat16))
+    taps = np.stack([np.stack([synthesis[h][rows] * tap_scale for h in range(2)])
+                     for rows in (x_rows, z_rows)])
+    return (np.stack(analysis), np.stack(synthesis).astype(jnp.bfloat16), taps.astype(jnp.bfloat16))
 
 
 def split(value):
@@ -40,11 +42,11 @@
 
 
 def kernel(tiles, count_ref, ana_hbm, syn_hbm, tsyn_hbm, x_hbm, g_hbm, w_hbm,
-           out_hbm, tap_hbm,
-           ana_ref, syn_ref, tsyn_ref, gbuf, xbuf, obuf, from_left, from_right, wbuf,
-           af, xf, wf, yf, tf, tap, pair_in, z_in, x_in, fin,
-           load_sem, out_sem, halo_s, halo_r, wz_s, wz_r, wx_s, wx_r, wp_s, wp_r,
-           p_s, p_r, z_s, z_r, x_s, x_r):
+           out_ref, tap_out,
+           ana_ref, syn_ref, tsyn_ref, live_ref, gbuf, xbuf, from_left, from_right, wbuf,
+           af, xf, wf, ya, yb, tf, tap, pair_in, q_in, e_in, z_in, x_in, fin,
+           load_sem, halo_s, halo_r, wz_s, wz_r, wx_s, wx_r, wp_s, wp_r,
+           p_s, p_r, q_s, q_r, e_s, e_r, h_s, h_r, z_s, z_r, x_s, x_r):
     live_count = count_ref[0, 0]
     ctx = lax.axis_index("ctx")
     rep = lax.axis_index("rep")
@@ -54,6 +56,7 @@
     xlo = lax.div(ctx, 8)
     chunks = tiles // 2
     half_cols = chunks * TILE
+    x_first = tiles // 2
 
     def device(x_lo, z_at, core_at, rep_at):
         return {"ctx": x_lo * 8 + z_at * 2 + core_at, "rep": rep_at}
@@ -93,10 +96,6 @@
     def cols(i):
         return pl.ds(pl.multiple_of(i * TILE, TILE), TILE)
 
-    def live_rows(b):
-        rows = lax.broadcasted_iota(jnp.int32, (REACH, TILE), 0) + b * REACH
-        return rows < live_count
-
     def halo_right(i):
         return remote(gbuf.at[pl.ds(384, 128), cols(i)], from_left.at[i],
                       halo_s.at[0, i], halo_r.at[0, i], right)
@@ -140,37 +139,85 @@
     def pair_copy(i):
         return remote(tap.at[i, 1 - core], pair_in.at[i], p_s.at[i], p_r.at[i], sibling)
 
+    def quarter_copy(i, d):
+        h = (1 - xlo, 1 - xlo, xlo)[d]
+        half = (rep, 1 - rep, 1 - rep)[d]
+        return remote(tap.at[i, core, pl.ds((h * 2 + half) * 2, 2)], q_in.at[i, d],
+                      q_s.at[i, d], q_r.at[i, d], x_peers[d])
+
+    def eighth(i, z_at):
+        rows = pl.ds(pl.multiple_of(lax.rem(z_at, 2) * 8, 8), 8)
+        return tap.at[i, core, (xlo * 2 + rep) * 2 + lax.div(z_at, 2), rows]
+
+    def eighth_copy(i, d):
+        return remote(eighth(i, lax.rem(z + 1 + d, Z)), e_in.at[i, d],
+                      e_s.at[i, d], e_r.at[i, d], z_peers[d])
+
+    def swap_copy(i, which):
+        part = fin.at[pl.ds(pl.multiple_of(which * 8, 8), 8), cols(i)]
+        return remote(part, part, h_s.at[i], h_r.at[i], x_far)
+
+    def stage_quarter(i):
+        for d in range(3):
+            quarter_copy(i, d).wait_recv()
+        mine = pl.ds((xlo * 2 + rep) * 2, 2)
+        tap[i, core, mine] = (tap[i, core, mine] + q_in[i, 0]) + (q_in[i, 1] + q_in[i, 2])
+        for d in range(Z - 1):
+            eighth_copy(i, d).start()
+
+    def stage_eighth(i):
+        for d in range(Z - 1):
+            eighth_copy(i, d).wait_recv()
+        total = (eighth(i, z)[...] + e_in[i, 0]) + (e_in[i, 1] + e_in[i, 2])
+        fin[pl.ds(pl.multiple_of(rep * 8, 8), 8), cols(i)] = total
+        swap_copy(i, rep).start()
+
     def z_copy(i, d):
-        return remote(tap.at[i, core, lax.rem(z + 1 + d, Z)], z_in.at[i, d],
-                      z_s.at[i, d], z_r.at[i, d], z_peers[d])
+        piece = pl.ds(lax.rem(z + 1 + d, Z) * 2, 2)
+        at = i - x_first
+        return remote(tap.at[i, core, piece], z_in.at[at, d], z_s.at[at, d], z_r.at[at, d], z_peers[d])
 
     def x_copy(i, d):
         h = (1 - xlo, 1 - xlo, xlo)[d]
-        return remote(tap.at[i, core, z, h], x_in.at[i, d], x_s.at[i, d], x_r.at[i, d], x_peers[d])
+        at = i - x_first
+        return remote(tap.at[i, core, z * 2 + h], x_in.at[at, d], x_s.at[at, d], x_r.at[at, d], x_peers[d])
 
     def stage_pair(i):
         pair_copy(i).wait_recv()
         tap[i, core] += pair_in[i]
-        for d in range(Z - 1):
-            z_copy(i, d).start()
+
+        @pl.when(i < x_first)
+        def _():
+            for d in range(3):
+                quarter_copy(i, d).start()
+
+        @pl.when(i >= x_first)
+        def _():
+            for d in range(Z - 1):
+                z_copy(i, d).start()
 
     def stage_z(i):
+        at = i - x_first
         for d in range(Z - 1):
             z_copy(i, d).wait_recv()
-        tap[i, core, z] = (tap[i, core, z] + z_in[i, 0]) + (z_in[i, 1] + z_in[i, 2])
+        mine = pl.ds(z * 2, 2)
+        tap[i, core, mine] = (tap[i, core, mine] + z_in[at, 0]) + (z_in[at, 1] + z_in[at, 2])
         for d in range(3):
             x_copy(i, d).start()
 
     def stage_x(i):
+        at = i - x_first
         for d in range(3):
             x_copy(i, d).wait_recv()
-        fin[:, cols(i)] = (tap[i, core, z, xlo] + x_in[i, 2]) + (x_in[i, 0] + x_in[i, 1])
-
+        fin[:, cols(i)] = (tap[i, core, z * 2 + xlo] + x_in[at, 2]) + (x_in[at, 0] + x_in[at, 1])
+
+    for b in range(4):
+        rows = lax.broadcasted_iota(jnp.int32, (REACH, TILE), 0) + b * REACH
+        live_ref[pl.ds(b * REACH, REACH), :] = jnp.where(rows < live_count, 1.0, 0.0).astype(jnp.bfloat16)
     loads[0].wait()
-    tail_live = live_rows(3)
 
     def mask_tail(i, carry):
-        gbuf[pl.ds(384, 128), cols(i)] = jnp.where(tail_live, gbuf[pl.ds(384, 128), cols(i)], 0)
+        gbuf[pl.ds(384, 128), cols(i)] = gbuf[pl.ds(384, 128), cols(i)] * live_ref[pl.ds(384, 128), :]
         return carry
 
     lax.fori_loop(0, tiles, mask_tail, None)
@@ -211,16 +258,19 @@
         high, low = split(value)
         ref[at, pl.ds(row, STEP), :] = high
         ref[at, pl.ds(256 + row, STEP), :] = low
-        ref[at, pl.ds(512 + row, STEP), :] = high
+
+    def synthesise(table, spectrum, at):
+        terms = jnp.concatenate([spectrum[at], spectrum[at, pl.ds(0, 256), :]], 0)
+        return jnp.dot(table, terms, preferred_element_type=jnp.float32)
 
     def own_tile(i, carry):
         for b in range(4):
             rows = pl.ds(b * REACH, REACH)
             g_block, x_block = gbuf[rows, cols(i)], xbuf[rows, cols(i)]
             if b > 0:
-                x_block = jnp.where(live_rows(b), x_block, 0)
+                x_block = x_block * live_ref[rows, :]
             if b in (1, 2):
-                g_block = jnp.where(live_rows(b), g_block, 0)
+                g_block = g_block * live_ref[rows, :]
             af[i, b + 1] = analyse(b + 1, g_block)
             xf[i, b] = analyse(b, x_block)
         return carry
@@ -269,90 +319,109 @@
 
         lax.fori_loop(0, 128 // STEP, chunk, None, unroll=True)
         for h in range(2):
-            terms = jnp.dot(tsyn_ref[h], tf[h], preferred_element_type=jnp.float32)
+            kind = jnp.where(i < x_first, 0, 1)
+            terms = synthesise(tsyn_ref[kind, h], tf, h)
             for core_at in range(2):
-                for z_at in range(Z):
-                    start = (core_at * Z + z_at) * 16
-                    tap[i, core_at, z_at, h] = terms[start:start + 16]
+                for u in range(4):
+                    start = core_at * 64 + u * 16
+                    unit = jnp.where(i < x_first, h * 4 + u, u * 2 + h)
+                    tap[i, core_at, unit] = terms[start:start + 16]
         pair_copy(i).start()
 
         @pl.when(i >= 1)
         def _():
             stage_pair(i - 1)
 
-        for c in range(min(2, chunks)):
-            @pl.when(i == tiles - 2 + c)
-            def _(c=c):
-                taps_forward(c)
+        @pl.when(i == tiles - 1)
+        def _():
+            taps_forward(0)
 
         return carry
 
     lax.fori_loop(0, tiles, tap_tile, None)
     stage_pair(tiles - 1)
-
-    def store_out(i):
-        return pltpu.make_async_copy(obuf.at[:, cols(i)], out_hbm.at[0, :, cols(i)], out_sem.at[i])
-
-    def grad_tile(k, carry):
-        chunk_at = lax.div(k, 2)
-        i = lax.rem(k, 2) * chunks + chunk_at
-
-        @pl.when(lax.rem(k, 2) == 0)
-        def _():
-            for half in range(2):
-                taps_pair(chunk_at, half, 1 - core).wait_recv()
-
-        for h in range(2):
-            block = wbuf[h, :, :, :, cols(i)].reshape(REACH, TILE)
-            wf[h] = analyse(h, block)
-
+    if chunks > 1:
+        taps_forward(1)
+
+    def weigh(i, at, spectrum):
         def chunk(c, carry):
             row = pl.multiple_of(c * STEP, STEP)
             re, im = pl.ds(row, STEP), pl.ds(128 + row, STEP)
             gr, gi = windows(i, re, im)
-            w0r, w0i = wf[0, re, :], wf[0, im, :]
-            w1r, w1i = wf[1, re, :], wf[1, im, :]
+            w0r, w0i = wf[at, re, :], wf[at, im, :]
+            w1r, w1i = wf[at + 1, re, :], wf[at + 1, im, :]
             for b in range(4):
                 yr = (w0r * gr[b] + w0i * gi[b]) + (w1r * gr[b + 1] + w1i * gi[b + 1])
                 yi = (w0r * gi[b] - w0i * gr[b]) + (w1r * gi[b + 1] - w1i * gr[b + 1])
-                put(yf, b, row, yr)
-                put(yf, b, 128 + row, yi)
+                put(spectrum, b, row, yr)
+                put(spectrum, b, 128 + row, yi)
             return carry
 
         lax.fori_loop(0, 128 // STEP, chunk, None, unroll=True)
+
+    def emit(i, spectrum):
         for b in range(4):
-            value = jnp.dot(syn_ref[b], yf[b], preferred_element_type=jnp.float32)
+            rows = pl.ds(b * REACH, REACH)
+            value = synthesise(syn_ref[b], spectrum, b).astype(jnp.bfloat16)
             if b > 0:
-                value = jnp.where(live_rows(b), value, 0)
-            obuf[pl.ds(b * REACH, REACH), cols(i)] = value.astype(jnp.bfloat16)
-        store_out(i).start()
-        @pl.when(jnp.logical_and(lax.rem(k, 2) == 1, chunk_at + 2 < chunks))
-        def _():
-            taps_forward(chunk_at + 2)
-
-        @pl.when(k >= 1)
-        def _():
-            stage_z(k - 1)
+                value = value * live_ref[rows, :]
+            out_ref[0, rows, cols(i)] = value
+
+    def grad_tiles(c, carry):
+        for half in range(2):
+            taps_pair(c, half, 1 - core).wait_recv()
+        first, second = c, chunks + c
+        for half, i in ((0, first), (1, second)):
+            for h in range(2):
+                block = wbuf[h, :, :, :, cols(i)].reshape(REACH, TILE)
+                wf[half * 2 + h] = analyse(h, block)
+        weigh(first, 0, ya)
+        weigh(second, 2, yb)
+        emit(first, ya)
+        emit(second, yb)
+
+        @pl.when(c + 2 < chunks)
+        def _():
+            taps_forward(c + 2)
+
+        @pl.when(c < 2)
+        def _():
+            for part in range(x_first // 2):
+                stage_quarter(c * (x_first // 2) + part)
+
+        @pl.when(c >= 2)
+        def _():
+            for part in range(x_first // 2):
+                stage_eighth((c - 2) * (x_first // 2) + part)
+
+        @pl.when(c >= 1)
+        def _():
+            stage_z(x_first + c - 1)
 
         return carry
 
-    lax.fori_loop(0, tiles, grad_tile, None)
+    lax.fori_loop(0, chunks, grad_tiles, None)
     stage_z(tiles - 1)
-
-    def total(i, carry):
-        stage_x(i)
-        return carry
-
-    lax.fori_loop(0, tiles, total, None)
-    last = pltpu.make_async_copy(fin, tap_hbm, load_sem.at[7])
-    last.start()
+    for i in range(x_first):
+        stage_x(x_first + i)
+        swap_copy(i, 1 - rep).wait_recv()
+    tap_out[...] = fin[...]
 
     def finish(i, carry):
-        store_out(i).wait()
         pair_copy(i).wait_send()
-        for d in range(3):
-            z_copy(i, d).wait_send()
-            x_copy(i, d).wait_send()
+
+        @pl.when(i < x_first)
+        def _():
+            for d in range(3):
+                quarter_copy(i, d).wait_send()
+                eighth_copy(i, d).wait_send()
+            swap_copy(i, rep).wait_send()
+
+        @pl.when(i >= x_first)
+        def _():
+            for d in range(3):
+                z_copy(i, d).wait_send()
+                x_copy(i, d).wait_send()
 
         @pl.when(ctx < ends - 1)
         def _():
@@ -372,7 +441,6 @@
             taps_x(c, d).wait_send()
         for half in range(2):
             taps_pair(c, half, core).wait_send()
-    last.wait()
 
 
 def fused(counts, x, g, taps):
@@ -382,17 +450,18 @@
     dma = pltpu.SemaphoreType.DMA
     hbm = pl.BlockSpec(memory_space=pl.ANY)
     f32, bf16 = jnp.float32, jnp.bfloat16
+    vmem = pl.BlockSpec(memory_space=pltpu.VMEM)
+    first, rest = tiles // 2, tiles - tiles // 2
     return pl.pallas_call(
         functools.partial(kernel, tiles),
-        out_shape=(jax.ShapeDtypeStruct(x.shape, bf16),
-                   jax.ShapeDtypeStruct(taps.shape, f32)),
+        out_shape=(pltpu.VMEM(x.shape, bf16), pltpu.VMEM(taps.shape, f32)),
         in_specs=[pl.BlockSpec(memory_space=pltpu.SMEM)] + [hbm] * 6,
-        out_specs=(hbm, hbm),
+        out_specs=(vmem, vmem),
         scratch_shapes=[
             pltpu.VMEM(ana.shape, bf16),
             pltpu.VMEM(syn.shape, bf16),
             pltpu.VMEM(tsyn.shape, bf16),
-            pltpu.VMEM((rows, channels), bf16),
+            pltpu.VMEM((rows, TILE), bf16),
             pltpu.VMEM((rows, channels), bf16),
             pltpu.VMEM((rows, channels), bf16),
             pltpu.VMEM((tiles, REACH, TILE), bf16),
@@ -400,22 +469,28 @@
             pltpu.VMEM((2, Z, 2, 16, channels), bf16),
             pltpu.VMEM((tiles, 6, 256, TILE), f32),
             pltpu.VMEM((tiles, 4, 256, TILE), f32),
-            pltpu.VMEM((2, 256, TILE), f32),
-            pltpu.VMEM((4, 768, TILE), bf16),
-            pltpu.VMEM((2, 768, TILE), bf16),
-            pltpu.VMEM((tiles, 2, Z, 2, 16, TILE), f32),
-            pltpu.VMEM((tiles, Z, 2, 16, TILE), f32),
-            pltpu.VMEM((tiles, 3, 2, 16, TILE), f32),
-            pltpu.VMEM((tiles, 3, 16, TILE), f32),
+            pltpu.VMEM((4, 256, TILE), f32),
+            pltpu.VMEM((4, 512, TILE), bf16),
+            pltpu.VMEM((4, 512, TILE), bf16),
+            pltpu.VMEM((2, 512, TILE), bf16),
+            pltpu.VMEM((tiles, 2, 8, 16, TILE), f32),
+            pltpu.VMEM((tiles, 8, 16, TILE), f32),
+            pltpu.VMEM((first, 3, 2, 16, TILE), f32),
+            pltpu.VMEM((first, 3, 8, TILE), f32),
+            pltpu.VMEM((rest, 3, 2, 16, TILE), f32),
+            pltpu.VMEM((rest, 3, 16, TILE), f32),
             pltpu.VMEM((16, channels), f32),
-            dma((8,)), dma((tiles,)),
+            dma((8,)),
             dma((2, tiles)), dma((2, tiles)),
             dma((3,)), dma((3,)),
             dma((tiles // 2, 3)), dma((tiles // 2, 3)),
             dma((tiles // 2, 2)), dma((tiles // 2, 2)),
             dma((tiles,)), dma((tiles,)),
-            dma((tiles, 3)), dma((tiles, 3)),
-            dma((tiles, 3)), dma((tiles, 3)),
+            dma((first, 3)), dma((first, 3)),
+            dma((first, 3)), dma((first, 3)),
+            dma((first,)), dma((first,)),
+            dma((rest, 3)), dma((rest, 3)),
+            dma((rest, 3)), dma((rest, 3)),
         ],
         compiler_params=pltpu.CompilerParams(
             collective_id=0, has_side_effects=True, vmem_limit_bytes=56 << 20),

time: 41.9 us -> 40.4 us (0.964)
  local copies, waits for them, and re-layouts: 3.85 us -> 1.98 us
    unnamed x4 -> x2, local copies, waits for them, and re-layouts: 3.85 us -> 1.98 us
where the time goes in v4:
time: 40.4 us; the launch traced here: 40.2 us
  Pallas kernels  37 us (92%)
  local copies, waits for them, and re-layouts  1.98 us (5%)
  between operations  1.29 us (3%)
    pallas_call x1, Pallas kernels, fused(): pl.pallas_call(functools.partial(kernel, tiles), out_shape=(pltpu.VMEM(x....  37 us
    unnamed x2, local copies, waits for them, and re-layouts  1.98 us

profile of v4, /device:TPU:0, one launch (start us, length us, event | category | flops | bytes accessed | tf_op | source)
XLA Modules:
  0.0 40.2 jit_solution(3227839462768236383)
XLA Ops:
  1.3 37.0 %shard_map.86 = (bf16[1,512,2048]{2,1,0:T(8,128)(2,1)S(1)}, f32[16,2048]{1,0:T(8,128)S(1)}) custom-call(s32[1,1]{1,0:T(1,128)S(6)} %copy.13.count_ref, bf16[4,256,256]{2,1,0:T(8,128)(2,1)} %constant.6.clone.ana_hbm, bf16[4,128,768]{2,1,0:T(8,128)(2,1)} %constant.7.clone.syn_hbm, bf16[2,2,128,768]{3,2,1,0:T(8,128)(2,1)} %constant.8.clone.tsyn_hbm, ...), custom_call_target="tpu_custom_call" | custom-call | tf_op jit(solution)/shard_map/pallas_call | solution.py:455
  38.3 1.3 %copy.11 = bf16[1,512,2048]{2,1,0:T(8,128)(2,1)} copy(bf16[1,512,2048]{2,1,0:T(8,128)(2,1)S(1)} %get-tuple-element.2) | data formatting | bytes 4194304
  39.6 0.7 %copy.12 = f32[16,2048]{1,0:T(8,128)} copy(f32[16,2048]{1,0:T(8,128)S(1)} %get-tuple-element.3) | data formatting | bytes 262144

commit v5 on v4

--- a/solution.py
+++ b/solution.py
@@ -12,6 +12,8 @@
 REACH = 128
 TILE = 256
 STEP = 16
+X_FIRST = 3
+HALO_FROM = 2
 Z = 4
 
 
@@ -35,6 +37,18 @@
     return (np.stack(analysis), np.stack(synthesis).astype(jnp.bfloat16), taps.astype(jnp.bfloat16))
 
 
+def reduction_plan(tiles, x_first, chunks):
+    early, late = list(range(x_first)), list(range(x_first, tiles))
+    cut = (x_first + 1) // 2
+    plan = [[("quarter", i) for i in early[:cut]] + [("z", i) for i in late[:1]],
+            [("quarter", i) for i in early[cut:]] + [("z", i) for i in late[1:2]],
+            [("eighth", i) for i in early[:cut]] + [("z", i) for i in late[2:3]],
+            [("eighth", i) for i in early[cut:]] + [("z", i) for i in late[3:4]],
+            [("z", i) for i in late[4:]] + [("x", i) for i in late] + [("swap", i) for i in early]]
+    assert len(plan) == chunks + 1
+    return plan
+
+
 def split(value):
     high = value.astype(jnp.bfloat16)
     low = (value - high.astype(jnp.float32)).astype(jnp.bfloat16)
@@ -55,8 +69,7 @@
     z = lax.rem(lax.div(ctx, 2), Z)
     xlo = lax.div(ctx, 8)
     chunks = tiles // 2
-    half_cols = chunks * TILE
-    x_first = tiles // 2
+    x_first = X_FIRST
 
     def device(x_lo, z_at, core_at, rep_at):
         return {"ctx": x_lo * 8 + z_at * 2 + core_at, "rep": rep_at}
@@ -80,10 +93,9 @@
     for peer in peers:
         pl.semaphore_signal(barrier, inc=1, device_id=peer, device_id_type=pl.DeviceIdType.MESH)
 
-    own_half = pl.ds(pl.multiple_of(rep * half_cols, TILE // 2), half_cols)
     loads = [
         pltpu.make_async_copy(g_hbm.at[0, pl.ds(384, 128), :], gbuf.at[pl.ds(384, 128), :], load_sem.at[0]),
-        pltpu.make_async_copy(w_hbm.at[:, own_half], wbuf.at[xlo, z, core, :, own_half], load_sem.at[1]),
+        pltpu.make_async_copy(w_hbm, wbuf.at[xlo, z, core], load_sem.at[1]),
         pltpu.make_async_copy(g_hbm.at[0, pl.ds(0, 384), :], gbuf.at[pl.ds(0, 384), :], load_sem.at[2]),
         pltpu.make_async_copy(x_hbm.at[0], xbuf, load_sem.at[3]),
         pltpu.make_async_copy(ana_hbm, ana_ref, load_sem.at[4]),
@@ -96,6 +108,10 @@
     def cols(i):
         return pl.ds(pl.multiple_of(i * TILE, TILE), TILE)
 
+    def tile_at(slot):
+        mixed = lax.rem(slot, 2) * x_first + lax.div(slot, 2)
+        return jnp.where(slot < 2 * x_first, mixed, slot)
+
     def halo_right(i):
         return remote(gbuf.at[pl.ds(384, 128), cols(i)], from_left.at[i],
                       halo_s.at[0, i], halo_r.at[0, i], right)
@@ -104,37 +120,36 @@
         return remote(g_hbm.at[0, pl.ds(0, 128), cols(i)], from_right.at[i],
                       halo_s.at[1, i], halo_r.at[1, i], left)
 
-    def taps_z(d):
-        return remote(w_hbm.at[:, own_half], wbuf.at[xlo, z, core, :, own_half],
-                      wz_s.at[d], wz_r.at[d], z_peers[d])
-
-    def taps_z_arrival(d):
+    def pair_cols(c):
+        return pl.ds(pl.multiple_of(c * 2 * TILE, 2 * TILE), 2 * TILE)
+
+    def taps_z(c, d):
+        return remote(w_hbm.at[:, pair_cols(c)], wbuf.at[xlo, z, core, :, pair_cols(c)],
+                      wz_s.at[c, d], wz_r.at[c, d], z_peers[d])
+
+    def taps_z_arrival(c, d):
         source = lax.rem(z + Z - 1 - d, Z)
-        return remote(w_hbm.at[:, own_half], wbuf.at[xlo, source, core, :, own_half],
-                      wz_s.at[d], wz_r.at[d], z_peers[d])
-
-    def half_tile(half, c):
-        return pl.ds(pl.multiple_of((half * chunks + c) * TILE, TILE), TILE)
-
-    def taps_x(c, d):
-        part = wbuf.at[xlo, :, core, :, half_tile(rep, c)]
+        return remote(w_hbm.at[:, pair_cols(c)], wbuf.at[xlo, source, core, :, pair_cols(c)],
+                      wz_s.at[c, d], wz_r.at[c, d], z_peers[d])
+
+    def taps_x(c, d, which):
+        part = wbuf.at[which, :, core, :, cols(2 * c + d)]
         return remote(part, part, wx_s.at[c, d], wx_r.at[c, d], x_peers[d])
 
-    def taps_x_arrival(c, d):
-        x_from = (1 - xlo, 1 - xlo, xlo)[d]
-        half_from = (rep, 1 - rep, 1 - rep)[d]
-        part = wbuf.at[x_from, :, core, :, half_tile(half_from, c)]
-        return remote(part, part, wx_s.at[c, d], wx_r.at[c, d], x_peers[d])
-
-    def taps_pair(c, half, which):
-        part = wbuf.at[:, :, which, :, half_tile(half, c)]
-        return remote(part, part, wp_s.at[c, half], wp_r.at[c, half], sibling)
-
-    def taps_forward(c):
-        for d in range(3):
-            taps_x_arrival(c, d).wait_recv()
-        for half in range(2):
-            taps_pair(c, half, core).start()
+    def taps_pair(c, which):
+        part = wbuf.at[:, :, which, :, pair_cols(c)]
+        return remote(part, part, wp_s.at[c], wp_r.at[c], sibling)
+
+    def taps_to_x(c):
+        for d in range(Z - 1):
+            taps_z_arrival(c, d).wait_recv()
+        for d in range(2):
+            taps_x(c, d, xlo).start()
+
+    def taps_to_pair(c):
+        for d in range(2):
+            taps_x(c, d, 1 - xlo).wait_recv()
+        taps_pair(c, core).start()
 
     def pair_copy(i):
         return remote(tap.at[i, 1 - core], pair_in.at[i], p_s.at[i], p_r.at[i], sibling)
@@ -181,6 +196,9 @@
         h = (1 - xlo, 1 - xlo, xlo)[d]
         at = i - x_first
         return remote(tap.at[i, core, z * 2 + h], x_in.at[at, d], x_s.at[at, d], x_r.at[at, d], x_peers[d])
+
+    def stage_swap(i):
+        swap_copy(i, 1 - rep).wait_recv()
 
     def stage_pair(i):
         pair_copy(i).wait_recv()
@@ -223,7 +241,9 @@
     lax.fori_loop(0, tiles, mask_tail, None)
     pl.semaphore_wait(barrier, len(peers))
 
-    def send_halo(i, carry):
+    def send_halo(slot):
+        i = tile_at(slot)
+
         @pl.when(ctx < ends - 1)
         def _():
             halo_right(i).start()
@@ -232,12 +252,9 @@
         def _():
             halo_left(i).start()
 
-        return carry
-
-    send_halo(0, None)
-    for d in range(Z - 1):
-        taps_z(d).start()
-    lax.fori_loop(1, tiles, send_halo, None)
+    for c in range(chunks):
+        for d in range(Z - 1):
+            taps_z(c, d).start()
 
     @pl.when(ctx == 0)
     def _():
@@ -273,15 +290,20 @@
                 g_block = g_block * live_ref[rows, :]
             af[i, b + 1] = analyse(b + 1, g_block)
             xf[i, b] = analyse(b, x_block)
+
+        for part in range(2):
+            slot = 2 * (i - HALO_FROM) + part
+
+            @pl.when(jnp.logical_and(slot >= 0, slot < tiles))
+            def _(slot=slot):
+                send_halo(slot)
+
         return carry
 
     lax.fori_loop(0, tiles, own_tile, None)
     loads[1].wait()
-    for d in range(Z - 1):
-        taps_z_arrival(d).wait_recv()
     for c in range(chunks):
-        for d in range(3):
-            taps_x(c, d).start()
+        taps_to_x(c)
     loads[5].wait()
     loads[6].wait()
 
@@ -290,7 +312,9 @@
         ai = [af[i, b, im, :] for b in range(6)]
         return [ar[b] + ar[b + 1] for b in range(5)], [ai[b] + ai[b + 1] for b in range(5)]
 
-    def tap_tile(i, carry):
+    def tap_tile(slot, carry):
+        i = tile_at(slot)
+
         @pl.when(ctx > 0)
         def _():
             halo_right(i).wait_recv()
@@ -328,20 +352,24 @@
                     tap[i, core_at, unit] = terms[start:start + 16]
         pair_copy(i).start()
 
-        @pl.when(i >= 1)
-        def _():
-            stage_pair(i - 1)
-
-        @pl.when(i == tiles - 1)
-        def _():
-            taps_forward(0)
+        @pl.when(slot >= 1)
+        def _():
+            stage_pair(tile_at(slot - 1))
+
+        @pl.when(slot >= tiles - 2)
+        def _():
+            taps_to_pair(slot - (tiles - 2))
 
         return carry
 
     lax.fori_loop(0, tiles, tap_tile, None)
     stage_pair(tiles - 1)
-    if chunks > 1:
-        taps_forward(1)
+    for c in range(2, chunks):
+        taps_to_pair(c)
+
+    stages = {"quarter": stage_quarter, "eighth": stage_eighth, "swap": stage_swap,
+              "z": stage_z, "x": stage_x}
+    plan = reduction_plan(tiles, x_first, chunks)
 
     def weigh(i, at, spectrum):
         def chunk(c, carry):
@@ -368,9 +396,8 @@
             out_ref[0, rows, cols(i)] = value
 
     def grad_tiles(c, carry):
-        for half in range(2):
-            taps_pair(c, half, 1 - core).wait_recv()
-        first, second = c, chunks + c
+        taps_pair(c, 1 - core).wait_recv()
+        first, second = 2 * c, 2 * c + 1
         for half, i in ((0, first), (1, second)):
             for h in range(2):
                 block = wbuf[h, :, :, :, cols(i)].reshape(REACH, TILE)
@@ -380,31 +407,17 @@
         emit(first, ya)
         emit(second, yb)
 
-        @pl.when(c + 2 < chunks)
-        def _():
-            taps_forward(c + 2)
-
-        @pl.when(c < 2)
-        def _():
-            for part in range(x_first // 2):
-                stage_quarter(c * (x_first // 2) + part)
-
-        @pl.when(c >= 2)
-        def _():
-            for part in range(x_first // 2):
-                stage_eighth((c - 2) * (x_first // 2) + part)
-
-        @pl.when(c >= 1)
-        def _():
-            stage_z(x_first + c - 1)
+        for at in range(chunks):
+            @pl.when(c == at)
+            def _(at=at):
+                for stage, tile in plan[at]:
+                    stages[stage](tile)
 
         return carry
 
     lax.fori_loop(0, chunks, grad_tiles, None)
-    stage_z(tiles - 1)
-    for i in range(x_first):
-        stage_x(x_first + i)
-        swap_copy(i, 1 - rep).wait_recv()
+    for stage, tile in plan[-1]:
+        stages[stage](tile)
     tap_out[...] = fin[...]
 
     def finish(i, carry):
@@ -434,13 +447,12 @@
         return carry
 
     lax.fori_loop(0, tiles, finish, None)
-    for d in range(3):
-        taps_z(d).wait_send()
     for c in range(chunks):
-        for d in range(3):
-            taps_x(c, d).wait_send()
-        for half in range(2):
-            taps_pair(c, half, core).wait_send()
+        for d in range(Z - 1):
+            taps_z(c, d).wait_send()
+        for d in range(2):
+            taps_x(c, d, xlo).wait_send()
+        taps_pair(c, core).wait_send()
 
 
 def fused(counts, x, g, taps):
@@ -451,7 +463,7 @@
     hbm = pl.BlockSpec(memory_space=pl.ANY)
     f32, bf16 = jnp.float32, jnp.bfloat16
     vmem = pl.BlockSpec(memory_space=pltpu.VMEM)
-    first, rest = tiles // 2, tiles - tiles // 2
+    first, rest = X_FIRST, tiles - X_FIRST
     return pl.pallas_call(
         functools.partial(kernel, tiles),
         out_shape=(pltpu.VMEM(x.shape, bf16), pltpu.VMEM(taps.shape, f32)),
@@ -482,9 +494,9 @@
             pltpu.VMEM((16, channels), f32),
             dma((8,)),
             dma((2, tiles)), dma((2, tiles)),
-            dma((3,)), dma((3,)),
             dma((tiles // 2, 3)), dma((tiles // 2, 3)),
             dma((tiles // 2, 2)), dma((tiles // 2, 2)),
+            dma((tiles // 2,)), dma((tiles // 2,)),
             dma((tiles,)), dma((tiles,)),
             dma((first, 3)), dma((first, 3)),
             dma((first, 3)), dma((first, 3)),

time: 40.4 us -> 37.6 us (0.931)
  Pallas kernels: 37 us -> 34.2 us
    pallas_call x1, Pallas kernels: 37 us -> 34.2 us  [fused(): pl.pallas_call(functools.partial(kernel, tiles), out_shape=(pltpu.VMEM(x....]
where the time goes in v5:
time: 37.6 us; the launch traced here: 37.5 us
  Pallas kernels  34.2 us (91%)
  local copies, waits for them, and re-layouts  1.98 us (5%)
  between operations  1.29 us (3%)
    pallas_call x1, Pallas kernels, fused(): pl.pallas_call(functools.partial(kernel, tiles), out_shape=(pltpu.VMEM(x....  34.2 us
    unnamed x2, local copies, waits for them, and re-layouts  1.98 us

profile of v5, /device:TPU:0, one launch (start us, length us, event | category | flops | bytes accessed | tf_op | source)
XLA Modules:
  0.0 37.5 jit_solution(13091634150518698457)
XLA Ops:
  1.3 34.2 %shard_map.86 = (bf16[1,512,2048]{2,1,0:T(8,128)(2,1)S(1)}, f32[16,2048]{1,0:T(8,128)S(1)}) custom-call(s32[1,1]{1,0:T(1,128)S(6)} %copy.13.count_ref, bf16[4,256,256]{2,1,0:T(8,128)(2,1)} %constant.6.clone.ana_hbm, bf16[4,128,768]{2,1,0:T(8,128)(2,1)} %constant.7.clone.syn_hbm, bf16[2,2,128,768]{3,2,1,0:T(8,128)(2,1)} %constant.8.clone.tsyn_hbm, ...), custom_call_target="tpu_custom_call" | custom-call | tf_op jit(solution)/shard_map/pallas_call | solution.py:467
  35.5 1.3 %copy.11 = bf16[1,512,2048]{2,1,0:T(8,128)(2,1)} copy(bf16[1,512,2048]{2,1,0:T(8,128)(2,1)S(1)} %get-tuple-element.2) | data formatting | bytes 4194304
  36.8 0.7 %copy.12 = f32[16,2048]{1,0:T(8,128)} copy(f32[16,2048]{1,0:T(8,128)S(1)} %get-tuple-element.3) | data formatting | bytes 262144

commit v6 on v5

--- a/solution.py
+++ b/solution.py
@@ -13,7 +13,7 @@
 TILE = 256
 STEP = 16
 X_FIRST = 3
-HALO_FROM = 2
+HALO_FROM = 0
 Z = 4
 
 
@@ -40,12 +40,15 @@
 def reduction_plan(tiles, x_first, chunks):
     early, late = list(range(x_first)), list(range(x_first, tiles))
     cut = (x_first + 1) // 2
-    plan = [[("quarter", i) for i in early[:cut]] + [("z", i) for i in late[:1]],
-            [("quarter", i) for i in early[cut:]] + [("z", i) for i in late[1:2]],
-            [("eighth", i) for i in early[:cut]] + [("z", i) for i in late[2:3]],
-            [("eighth", i) for i in early[cut:]] + [("z", i) for i in late[3:4]],
-            [("z", i) for i in late[4:]] + [("x", i) for i in late] + [("swap", i) for i in early]]
-    assert len(plan) == chunks + 1
+    plan = [[("z", i) for i in late[4:5]] + [("eighth", i) for i in early[:cut]],
+            [("eighth", i) for i in early[cut:]],
+            [],
+            [],
+            [("x", i) for i in late] + [("swap", i) for i in early],
+            [("quarter", i) for i in early[:cut]] + [("z", i) for i in late[:2]]
+            + [("quarter", i) for i in early[cut:]],
+            [("z", i) for i in late[2:4]]]
+    assert len(plan) == chunks + 3
     return plan
 
 
@@ -252,9 +255,6 @@
         def _():
             halo_left(i).start()
 
-    for c in range(chunks):
-        for d in range(Z - 1):
-            taps_z(c, d).start()
 
     @pl.when(ctx == 0)
     def _():
@@ -301,9 +301,10 @@
         return carry
 
     lax.fori_loop(0, tiles, own_tile, None)
+    for c in range(chunks):
+        for d in range(Z - 1):
+            taps_z(c, d).start()
     loads[1].wait()
-    for c in range(chunks):
-        taps_to_x(c)
     loads[5].wait()
     loads[6].wait()
 
@@ -352,24 +353,29 @@
                     tap[i, core_at, unit] = terms[start:start + 16]
         pair_copy(i).start()
 
-        @pl.when(slot >= 1)
-        def _():
-            stage_pair(tile_at(slot - 1))
-
-        @pl.when(slot >= tiles - 2)
-        def _():
-            taps_to_pair(slot - (tiles - 2))
+        @pl.when(slot >= 2)
+        def _():
+            stage_pair(tile_at(slot - 2))
+
 
         return carry
 
     lax.fori_loop(0, tiles, tap_tile, None)
-    stage_pair(tiles - 1)
-    for c in range(2, chunks):
-        taps_to_pair(c)
-
     stages = {"quarter": stage_quarter, "eighth": stage_eighth, "swap": stage_swap,
               "z": stage_z, "x": stage_x}
     plan = reduction_plan(tiles, x_first, chunks)
+
+    stage_pair(tiles - 2)
+    for c in range(chunks):
+        taps_to_x(c)
+    stage_pair(tiles - 1)
+    for stage, tile in plan[chunks + 1]:
+        stages[stage](tile)
+    for c in range(chunks):
+        taps_to_pair(c)
+    for stage, tile in plan[chunks + 2]:
+        stages[stage](tile)
+
 
     def weigh(i, at, spectrum):
         def chunk(c, carry):
@@ -416,7 +422,7 @@
         return carry
 
     lax.fori_loop(0, chunks, grad_tiles, None)
-    for stage, tile in plan[-1]:
+    for stage, tile in plan[chunks]:
         stages[stage](tile)
     tap_out[...] = fin[...]
 

time: 37.6 us -> 35.6 us (0.947)
  Pallas kernels: 34.2 us -> 32.1 us
    pallas_call x1, Pallas kernels: 34.2 us -> 32.1 us  [fused(): pl.pallas_call(functools.partial(kernel, tiles), out_shape=(pltpu.VMEM(x....]
where the time goes in v6:
time: 35.6 us; the launch traced here: 35.3 us
  Pallas kernels  32.1 us (90%)
  local copies, waits for them, and re-layouts  1.98 us (6%)
  between operations  1.29 us (4%)
    pallas_call x1, Pallas kernels, fused(): pl.pallas_call(functools.partial(kernel, tiles), out_shape=(pltpu.VMEM(x....  32.1 us
    unnamed x2, local copies, waits for them, and re-layouts  1.98 us

profile of v6, /device:TPU:0, one launch (start us, length us, event | category | flops | bytes accessed | tf_op | source)
XLA Modules:
  0.0 35.3 jit_solution(4452678512831001353)
XLA Ops:
  1.3 32.1 %shard_map.86 = (bf16[1,512,2048]{2,1,0:T(8,128)(2,1)S(1)}, f32[16,2048]{1,0:T(8,128)S(1)}) custom-call(s32[1,1]{1,0:T(1,128)S(6)} %copy.13.count_ref, bf16[4,256,256]{2,1,0:T(8,128)(2,1)} %constant.6.clone.ana_hbm, bf16[4,128,768]{2,1,0:T(8,128)(2,1)} %constant.7.clone.syn_hbm, bf16[2,2,128,768]{3,2,1,0:T(8,128)(2,1)} %constant.8.clone.tsyn_hbm, ...), custom_call_target="tpu_custom_call" | custom-call | tf_op jit(solution)/shard_map/pallas_call | solution.py:473
  33.3 1.3 %copy.11 = bf16[1,512,2048]{2,1,0:T(8,128)(2,1)} copy(bf16[1,512,2048]{2,1,0:T(8,128)(2,1)S(1)} %get-tuple-element.2) | data formatting | bytes 4194304
  34.7 0.7 %copy.12 = f32[16,2048]{1,0:T(8,128)} copy(f32[16,2048]{1,0:T(8,128)S(1)} %get-tuple-element.3) | data formatting | bytes 262144

commit v7 on v6

--- a/solution.py
+++ b/solution.py
@@ -366,9 +366,9 @@
     plan = reduction_plan(tiles, x_first, chunks)
 
     stage_pair(tiles - 2)
+    stage_pair(tiles - 1)
     for c in range(chunks):
         taps_to_x(c)
-    stage_pair(tiles - 1)
     for stage, tile in plan[chunks + 1]:
         stages[stage](tile)
     for c in range(chunks):

time: 35.6 us -> 35.8 us (level)
  no operation moved by 1% of the time
where the time goes in v7:
time: 35.8 us; the launch traced here: 35.3 us
  Pallas kernels  32.1 us (90%)
  local copies, waits for them, and re-layouts  1.98 us (6%)
  between operations  1.29 us (4%)
    pallas_call x1, Pallas kernels, fused(): pl.pallas_call(functools.partial(kernel, tiles), out_shape=(pltpu.VMEM(x....  32.1 us
    unnamed x2, local copies, waits for them, and re-layouts  1.98 us

profile of v7, /device:TPU:0, one launch (start us, length us, event | category | flops | bytes accessed | tf_op | source)
XLA Modules:
  0.0 35.3 jit_solution(10791527063183814689)
XLA Ops:
  1.3 32.1 %shard_map.86 = (bf16[1,512,2048]{2,1,0:T(8,128)(2,1)S(1)}, f32[16,2048]{1,0:T(8,128)S(1)}) custom-call(s32[1,1]{1,0:T(1,128)S(6)} %copy.13.count_ref, bf16[4,256,256]{2,1,0:T(8,128)(2,1)} %constant.6.clone.ana_hbm, bf16[4,128,768]{2,1,0:T(8,128)(2,1)} %constant.7.clone.syn_hbm, bf16[2,2,128,768]{3,2,1,0:T(8,128)(2,1)} %constant.8.clone.tsyn_hbm, ...), custom_call_target="tpu_custom_call" | custom-call | tf_op jit(solution)/shard_map/pallas_call | solution.py:473
  33.4 1.3 %copy.11 = bf16[1,512,2048]{2,1,0:T(8,128)(2,1)} copy(bf16[1,512,2048]{2,1,0:T(8,128)(2,1)S(1)} %get-tuple-element.2) | data formatting | bytes 4194304
  34.7 0.7 %copy.12 = f32[16,2048]{1,0:T(8,128)} copy(f32[16,2048]{1,0:T(8,128)S(1)} %get-tuple-element.3) | data formatting | bytes 262144
